TPU v7x, 32 devices: a whole 2x2x4 slice. The times are simulated.
32 devices in a mesh: section: 4 (over x, core), dp: 8 (over z, y).
Axes of the slice: x: 2, y: 2, z: 4, core: 2. Of those that a mesh axis runs over, the one named last changes fastest.
Arguments:
- images: bfloat16 [16, 256, 768], P('dp'), may hold values from -6 to 6
- cotangent: bfloat16 [16, 256, 768], P('dp'), may hold values from -6 to 6
- kept_count: int32 [16], P('dp'), may hold values from 1 to 256, as said below
- kept_index: int32 [16, 256], P('dp'), may hold values from 0 to 255, as said below
- gain_one: bfloat16 [4, 768], P('section', 'dp'), may hold values from 0.5 to 1.5
- shift_one: bfloat16 [4, 768], P('section', 'dp'), may hold values from -1.5 to 1.5
- qkv_matrix: bfloat16 [4, 768, 2304], P('section', 'dp'), may hold values from -0.21875 to 0.21875
- qkv_shift: bfloat16 [4, 2304], P('section', 'dp'), may hold values from -1.5 to 1.5
- proj_matrix: bfloat16 [4, 768, 768], P('section', 'dp'), may hold values from -0.625 to 0.625
- proj_shift: bfloat16 [4, 768], P('section', 'dp'), may hold values from -1.5 to 1.5
- gain_two: bfloat16 [4, 768], P('section', 'dp'), may hold values from 0.5 to 1.5
- shift_two: bfloat16 [4, 768], P('section', 'dp'), may hold values from -1.5 to 1.5
- up_matrix: bfloat16 [4, 768, 3072], P('section', 'dp'), may hold values from -0.21875 to 0.21875
- up_shift: bfloat16 [4, 3072], P('section', 'dp'), may hold values from -1.5 to 1.5
- down_matrix: bfloat16 [4, 3072, 768], P('section', 'dp'), may hold values from -0.109375 to 0.109375
- down_shift: bfloat16 [4, 768], P('section', 'dp'), may hold values from -1.5 to 1.5
- frequency: bfloat16 [4, 768], P('section', 'dp'), may hold values from 0.049804688 to 1
Outputs:
- section_outputs: float32 [4, 16, 256, 768], P('section', 'dp')
- section_input_grads: float32 [4, 16, 256, 768], P('section', 'dp')
- gain_one_grad: float32 [4, 768], P('section', 'dp')
- shift_one_grad: float32 [4, 768], P('section', 'dp')
- qkv_matrix_grad: float32 [4, 768, 2304], P('section', 'dp')
- qkv_shift_grad: float32 [4, 2304], P('section', 'dp')
- proj_matrix_grad: float32 [4, 768, 768], P('section', 'dp')
- proj_shift_grad: float32 [4, 768], P('section', 'dp')
- gain_two_grad: float32 [4, 768], P('section', 'dp')
- shift_two_grad: float32 [4, 768], P('section', 'dp')
- up_matrix_grad: float32 [4, 768, 3072], P('section', 'dp')
- up_shift_grad: float32 [4, 3072], P('section', 'dp')
- down_matrix_grad: float32 [4, 3072, 768], P('section', 'dp')
- down_shift_grad: float32 [4, 768], P('section', 'dp')
- frequency_grad: float32 [4, 768], P('section', 'dp')
Inputs may be any that keep to these rules, and one draw needn't show every extreme that they name: `kept_count`: every image keeps at least one patch, and some image keeps all 256. `kept_index`: each row is a permutation of the 256 grid indices: slots below the image's kept_count hold its kept patches in rising order, the later slots the dropped ones in rising order.
All inputs are finite; a program needn't handle non-finite values.
Results may differ from a plain program's by a relative error of at most 0.025.
Values may be sent and summed in bfloat16 or wider, within the bound.
A program may use at most 256 MiB of HBM per device.

v0:
```python
import jax
import jax.numpy as jnp
from jax import lax
from jax.sharding import PartitionSpec as P

D = 768
H = 12
HD = 64
GRID = 16
MICRO = 2
IMG_MB = 1


EPSILON = 1e-06
MASKED = -1e30


def shifted(value, axis, steps):
    count = lax.axis_size(axis)
    first, last = (max(0, -steps), min(count, count - steps))
    return lax.ppermute(value, axis, [(source, source + steps) for source in range(first, last)])


def layer_norm(values, gain_vector, shift_vector):
    row_mean = jnp.mean(values, axis=-1, keepdims=True)
    centred = values - row_mean
    variance = jnp.mean(centred * centred, axis=-1, keepdims=True)
    return centred * lax.rsqrt(variance + EPSILON) * gain_vector + shift_vector


def exact_gelu(values):
    return jax.nn.gelu(values, approximate=False)


def rotate(values, cosine, sine_part):
    half_width = values.shape[-1] // 2
    first_half = values[..., :half_width]
    second_half = values[..., half_width:]
    return jnp.concatenate(
        [
            first_half * cosine - second_half * sine_part,
            first_half * sine_part + second_half * cosine,
        ],
        axis=-1,
    )


def rope_pair(queries, keys_raw, freq_vector, row_pos, col_pos):
    half_width = HD // 2
    freq_rows = freq_vector[: D // 2].reshape(H, half_width)
    freq_cols = freq_vector[D // 2 :].reshape(H, half_width)
    angle = row_pos[:, :, None, None] * freq_rows + col_pos[:, :, None, None] * freq_cols
    cosine = jnp.cos(angle)
    sine_part = jnp.sin(angle)
    return (rotate(queries, cosine, sine_part), rotate(keys_raw, cosine, sine_part))


def positions(index_rows):
    return ((index_rows // GRID).astype(jnp.float32), (index_rows % GRID).astype(jnp.float32))


def attention_scores(low_q, low_k, keep_rows):
    scores = jnp.einsum(
        "bqhd,bkhd->bhqk", low_q, low_k, preferred_element_type=jnp.float32
    ) * HD ** (-0.5)
    return jnp.where(keep_rows[:, None, None, :] > 0, scores, MASKED)


def forward_block(section_in, keep_rows, index_rows, params):
    (
        gain_one,
        shift_one,
        qkv_matrix,
        qkv_shift,
        proj_matrix,
        proj_shift,
        gain_two,
        shift_two,
        up_matrix,
        up_shift,
        down_matrix,
        down_shift,
        frequency,
    ) = params
    images_here = section_in.shape[0]
    patches = section_in.shape[1]
    source = section_in.astype(jnp.float32)
    normed = layer_norm(source, gain_one.astype(jnp.float32), shift_one.astype(jnp.float32)).astype(
        jnp.bfloat16
    )
    mixed = jnp.dot(normed, qkv_matrix, preferred_element_type=jnp.float32) + qkv_shift.astype(
        jnp.float32
    )
    queries = mixed[..., :D].reshape(images_here, patches, H, HD)
    keys_raw = mixed[..., D : 2 * D].reshape(images_here, patches, H, HD)
    values_raw = mixed[..., 2 * D :].reshape(images_here, patches, H, HD)
    row_pos, col_pos = positions(index_rows)
    turned_q, turned_k = rope_pair(
        queries, keys_raw, frequency.astype(jnp.float32), row_pos, col_pos
    )
    low_q = turned_q.astype(jnp.bfloat16)
    low_k = turned_k.astype(jnp.bfloat16)
    low_v = values_raw.astype(jnp.bfloat16)
    scores = attention_scores(low_q, low_k, keep_rows)
    row_top = jnp.max(scores, axis=-1, keepdims=True)
    log_total = row_top + jnp.log(jnp.sum(jnp.exp(scores - row_top), axis=-1, keepdims=True))
    soft_rows = jnp.exp(scores - log_total).astype(jnp.bfloat16)
    attended = jnp.einsum("bhqk,bkhd->bqhd", soft_rows, low_v, preferred_element_type=jnp.float32)
    attended = attended.reshape(images_here, patches, D).astype(jnp.bfloat16)
    keep_col = keep_rows[..., None]
    branch_one = jnp.dot(
        attended, proj_matrix, preferred_element_type=jnp.float32
    ) + proj_shift.astype(jnp.float32)
    middle = source + keep_col * branch_one
    normed_two = layer_norm(
        middle, gain_two.astype(jnp.float32), shift_two.astype(jnp.float32)
    ).astype(jnp.bfloat16)
    hidden = jnp.dot(normed_two, up_matrix, preferred_element_type=jnp.float32) + up_shift.astype(
        jnp.float32
    )
    active = exact_gelu(hidden).astype(jnp.bfloat16)
    branch_two = jnp.dot(
        active, down_matrix, preferred_element_type=jnp.float32
    ) + down_shift.astype(jnp.float32)
    result = middle + keep_col * branch_two
    saved = (
        source,
        normed,
        queries,
        keys_raw,
        low_q,
        low_k,
        low_v,
        log_total,
        attended,
        middle,
        normed_two,
        hidden,
        active,
    )
    return (result, saved)


def backward_block(grad_out, keep_rows, index_rows, saved, params):
    (
        gain_one,
        shift_one,
        qkv_matrix,
        qkv_shift,
        proj_matrix,
        proj_shift,
        gain_two,
        shift_two,
        up_matrix,
        up_shift,
        down_matrix,
        down_shift,
        frequency,
    ) = params
    (
        source,
        normed,
        queries,
        keys_raw,
        low_q,
        low_k,
        low_v,
        log_total,
        attended,
        middle,
        normed_two,
        hidden,
        active,
    ) = saved
    images_here = grad_out.shape[0]
    patches = grad_out.shape[1]
    keep_col = keep_rows[..., None]
    grad_two = (grad_out * keep_col).astype(jnp.bfloat16)
    down_grad = jnp.einsum("bpf,bpd->fd", active, grad_two, preferred_element_type=jnp.float32)
    down_shift_grad = jnp.sum(grad_two.astype(jnp.float32), axis=(0, 1))
    grad_active = jnp.einsum(
        "bpd,fd->bpf", grad_two, down_matrix, preferred_element_type=jnp.float32
    )
    unused, gelu_pull = jax.vjp(exact_gelu, hidden)
    grad_hidden = gelu_pull(grad_active)[0].astype(jnp.bfloat16)
    up_grad = jnp.einsum("bpd,bpf->df", normed_two, grad_hidden, preferred_element_type=jnp.float32)
    up_shift_grad = jnp.sum(grad_hidden.astype(jnp.float32), axis=(0, 1))
    grad_normed_two = jnp.einsum(
        "bpf,df->bpd", grad_hidden, up_matrix, preferred_element_type=jnp.float32
    )
    unused, norm_pull = jax.vjp(
        layer_norm, middle, gain_two.astype(jnp.float32), shift_two.astype(jnp.float32)
    )
    grad_mid_part, gain_two_grad, shift_two_grad = norm_pull(grad_normed_two)
    grad_middle = grad_out + grad_mid_part
    grad_one = (grad_middle * keep_col).astype(jnp.bfloat16)
    proj_grad = jnp.einsum("bpi,bpo->io", attended, grad_one, preferred_element_type=jnp.float32)
    proj_shift_grad = jnp.sum(grad_one.astype(jnp.float32), axis=(0, 1))
    grad_attended = jnp.einsum(
        "bpo,io->bpi", grad_one, proj_matrix, preferred_element_type=jnp.float32
    )
    grad_attended = grad_attended.astype(jnp.bfloat16).reshape(images_here, patches, H, HD)
    scores = attention_scores(low_q, low_k, keep_rows)
    soft_exact = jnp.exp(scores - log_total)
    grad_soft = jnp.einsum(
        "bqhd,bkhd->bhqk", grad_attended, low_v, preferred_element_type=jnp.float32
    )
    grad_values = jnp.einsum(
        "bhqk,bqhd->bkhd",
        soft_exact.astype(jnp.bfloat16),
        grad_attended,
        preferred_element_type=jnp.float32,
    )
    centre = jnp.sum(soft_exact * grad_soft, axis=-1, keepdims=True)
    grad_scores = (soft_exact * (grad_soft - centre)).astype(jnp.bfloat16)
    score_scale = HD ** (-0.5)
    grad_turned_q = (
        jnp.einsum("bhqk,bkhd->bqhd", grad_scores, low_k, preferred_element_type=jnp.float32)
        * score_scale
    )
    grad_turned_k = (
        jnp.einsum("bhqk,bqhd->bkhd", grad_scores, low_q, preferred_element_type=jnp.float32)
        * score_scale
    )
    row_pos, col_pos = positions(index_rows)

    def turn_both(query_part, key_part, freq_part):
        return rope_pair(query_part, key_part, freq_part, row_pos, col_pos)

    unused, turn_pull = jax.vjp(turn_both, queries, keys_raw, frequency.astype(jnp.float32))
    grad_queries, grad_keys, frequency_grad = turn_pull((grad_turned_q, grad_turned_k))
    grad_mixed = jnp.concatenate(
        [
            grad_queries.reshape(images_here, patches, D),
            grad_keys.reshape(images_here, patches, D),
            grad_values.reshape(images_here, patches, D),
        ],
        axis=-1,
    ).astype(jnp.bfloat16)
    qkv_grad = jnp.einsum("bpd,bpe->de", normed, grad_mixed, preferred_element_type=jnp.float32)
    qkv_shift_grad = jnp.sum(grad_mixed.astype(jnp.float32), axis=(0, 1))
    grad_normed = jnp.einsum(
        "bpe,de->bpd", grad_mixed, qkv_matrix, preferred_element_type=jnp.float32
    )
    unused, first_pull = jax.vjp(
        layer_norm, source, gain_one.astype(jnp.float32), shift_one.astype(jnp.float32)
    )
    grad_source_part, gain_one_grad, shift_one_grad = first_pull(grad_normed)
    grad_input = grad_middle + grad_source_part
    grads = (
        gain_one_grad,
        shift_one_grad,
        qkv_grad,
        qkv_shift_grad,
        proj_grad,
        proj_shift_grad,
        gain_two_grad,
        shift_two_grad,
        up_grad,
        up_shift_grad,
        down_grad,
        down_shift_grad,
        frequency_grad,
    )
    return (grad_input, grads)


def local(
    images,
    cotangent,
    kept_count,
    kept_index,
    gain_one,
    shift_one,
    qkv_matrix,
    qkv_shift,
    proj_matrix,
    proj_shift,
    gain_two,
    shift_two,
    up_matrix,
    up_shift,
    down_matrix,
    down_shift,
    frequency,
):
    sections = lax.axis_size("section")
    section_no = lax.axis_index("section")
    gathered = (
        lax.all_gather(gain_one, "dp", axis=1, tiled=True),
        lax.all_gather(shift_one, "dp", axis=1, tiled=True),
        lax.all_gather(qkv_matrix, "dp", axis=1, tiled=True),
        lax.all_gather(qkv_shift, "dp", axis=1, tiled=True),
        lax.all_gather(proj_matrix, "dp", axis=1, tiled=True),
        lax.all_gather(proj_shift, "dp", axis=1, tiled=True),
        lax.all_gather(gain_two, "dp", axis=1, tiled=True),
        lax.all_gather(shift_two, "dp", axis=1, tiled=True),
        lax.all_gather(up_matrix, "dp", axis=1, tiled=True),
        lax.all_gather(up_shift, "dp", axis=1, tiled=True),
        lax.all_gather(down_matrix, "dp", axis=1, tiled=True),
        lax.all_gather(down_shift, "dp", axis=1, tiled=True),
        lax.all_gather(frequency, "dp", axis=1, tiled=True),
    )
    params = tuple((values[0] for values in gathered))
    shard_shapes = tuple(
        (
            values.shape
            for values in (
                gain_one,
                shift_one,
                qkv_matrix,
                qkv_shift,
                proj_matrix,
                proj_shift,
                gain_two,
                shift_two,
                up_matrix,
                up_shift,
                down_matrix,
                down_shift,
                frequency,
            )
        )
    )
    patches = images.shape[1]
    keep_all = (jnp.arange(patches)[None, :] < kept_count[:, None]).astype(jnp.float32)
    total_steps = MICRO + sections - 1
    incoming = jnp.zeros((IMG_MB, patches, D), jnp.bfloat16)
    outputs = jnp.zeros((MICRO * IMG_MB, patches, D), jnp.float32)
    kept_steps = []
    for moment in range(total_steps):
        batch_no = moment - section_no
        valid = (batch_no >= 0) & (batch_no < MICRO)
        start = jnp.clip(batch_no, 0, MICRO - 1) * IMG_MB
        if moment < MICRO:
            fresh = lax.slice_in_dim(images, moment * IMG_MB, (moment + 1) * IMG_MB, axis=0)
        else:
            fresh = jnp.zeros((IMG_MB, patches, D), jnp.bfloat16)
        section_in = jnp.where(section_no == 0, fresh, incoming)
        keep_rows = lax.dynamic_slice_in_dim(keep_all, start, IMG_MB, 0)
        index_rows = lax.dynamic_slice_in_dim(kept_index, start, IMG_MB, 0)
        result, saved = forward_block(section_in, keep_rows, index_rows, params)
        result_low = result.astype(jnp.bfloat16)
        kept_steps.append((section_in, keep_rows, index_rows))
        outputs = jnp.where(
            valid, lax.dynamic_update_slice_in_dim(outputs, result, start, 0), outputs
        )
        if moment < total_steps - 1:
            incoming = shifted(result_low, "section", 1)
    gathered = (
        lax.all_gather(gain_one, "dp", axis=1, tiled=True),
        lax.all_gather(shift_one, "dp", axis=1, tiled=True),
        lax.all_gather(qkv_matrix, "dp", axis=1, tiled=True),
        lax.all_gather(qkv_shift, "dp", axis=1, tiled=True),
        lax.all_gather(proj_matrix, "dp", axis=1, tiled=True),
        lax.all_gather(proj_shift, "dp", axis=1, tiled=True),
        lax.all_gather(gain_two, "dp", axis=1, tiled=True),
        lax.all_gather(shift_two, "dp", axis=1, tiled=True),
        lax.all_gather(up_matrix, "dp", axis=1, tiled=True),
        lax.all_gather(up_shift, "dp", axis=1, tiled=True),
        lax.all_gather(down_matrix, "dp", axis=1, tiled=True),
        lax.all_gather(down_shift, "dp", axis=1, tiled=True),
        lax.all_gather(frequency, "dp", axis=1, tiled=True),
    )
    params = tuple((values[0] for values in gathered))
    totals = tuple((jnp.zeros(values.shape, jnp.float32) for values in params))
    reduced = tuple((jnp.zeros(shape_now, jnp.float32) for shape_now in shard_shapes))
    incoming = jnp.zeros((IMG_MB, patches, D), jnp.bfloat16)
    input_grads = jnp.zeros((MICRO * IMG_MB, patches, D), jnp.float32)
    for moment in range(total_steps):
        earlier = total_steps - 1 - moment
        batch_no = earlier - section_no
        valid = (batch_no >= 0) & (batch_no < MICRO)
        start = jnp.clip(batch_no, 0, MICRO - 1) * IMG_MB
        from_next = jnp.where(
            section_no == sections - 1,
            lax.dynamic_slice_in_dim(cotangent, start, IMG_MB, 0),
            incoming,
        )
        grad_out = jnp.where(valid, from_next.astype(jnp.float32), 0.0)
        section_in, keep_rows, index_rows = kept_steps[earlier]
        saved = forward_block(section_in, keep_rows, index_rows, params)[1]
        grad_input, grads = backward_block(grad_out, keep_rows, index_rows, saved, params)
        totals = tuple((running + fresh_grad for running, fresh_grad in zip(totals, grads)))
        grad_low = grad_input.astype(jnp.bfloat16)
        input_grads = jnp.where(
            valid, lax.dynamic_update_slice_in_dim(input_grads, grad_input, start, 0), input_grads
        )
        if moment < total_steps - 1:
            incoming = shifted(grad_low, "section", -1)
    reduced = (
        lax.psum_scatter(totals[0][None], "dp", scatter_dimension=1, tiled=True),
        lax.psum_scatter(totals[1][None], "dp", scatter_dimension=1, tiled=True),
        lax.psum_scatter(totals[2][None], "dp", scatter_dimension=1, tiled=True),
        lax.psum_scatter(totals[3][None], "dp", scatter_dimension=1, tiled=True),
        lax.psum_scatter(totals[4][None], "dp", scatter_dimension=1, tiled=True),
        lax.psum_scatter(totals[5][None], "dp", scatter_dimension=1, tiled=True),
        lax.psum_scatter(totals[6][None], "dp", scatter_dimension=1, tiled=True),
        lax.psum_scatter(totals[7][None], "dp", scatter_dimension=1, tiled=True),
        lax.psum_scatter(totals[8][None], "dp", scatter_dimension=1, tiled=True),
        lax.psum_scatter(totals[9][None], "dp", scatter_dimension=1, tiled=True),
        lax.psum_scatter(totals[10][None], "dp", scatter_dimension=1, tiled=True),
        lax.psum_scatter(totals[11][None], "dp", scatter_dimension=1, tiled=True),
        lax.psum_scatter(totals[12][None], "dp", scatter_dimension=1, tiled=True),
    )
    return (
        outputs[None],
        input_grads[None],
        reduced[0],
        reduced[1],
        reduced[2],
        reduced[3],
        reduced[4],
        reduced[5],
        reduced[6],
        reduced[7],
        reduced[8],
        reduced[9],
        reduced[10],
        reduced[11],
        reduced[12],
    )


def solution(mesh):
    in_specs = (
        P("dp", None, None),
        P("dp", None, None),
        P("dp"),
        P("dp", None),
        P("section", "dp"),
        P("section", "dp"),
        P("section", "dp", None),
        P("section", "dp"),
        P("section", "dp", None),
        P("section", "dp"),
        P("section", "dp"),
        P("section", "dp"),
        P("section", "dp", None),
        P("section", "dp"),
        P("section", "dp", None),
        P("section", "dp"),
        P("section", "dp"),
    )
    out_specs = (
        P("section", "dp", None, None),
        P("section", "dp", None, None),
        P("section", "dp"),
        P("section", "dp"),
        P("section", "dp", None),
        P("section", "dp"),
        P("section", "dp", None),
        P("section", "dp"),
        P("section", "dp"),
        P("section", "dp"),
        P("section", "dp", None),
        P("section", "dp"),
        P("section", "dp", None),
        P("section", "dp"),
        P("section", "dp"),
    )
    return jax.shard_map(local, mesh=mesh, in_specs=in_specs, out_specs=out_specs, check_vma=False)
```

profile of v0, /device:TPU:17, one launch (start us, length us, event | category | flops | bytes accessed | tf_op | source)
XLA Modules:
  0.0 1760.3 jit_solution(2928940449756884143)
XLA Ops:
  19.4 25.2 %all-reduce.38 = (bf16[2304]{0:T(1024)(128)(2,1)S(1)}, bf16[768]{0:T(1024)(128)(2,1)S(1)}, bf16[768]{0:T(1024)(128)(2,1)S(1)}, bf16[768]{0:T(1024)(128)(2,1)S(1)...) all-reduce(bf16[2304]{0:T(1024)(128)(2,1)S(1)} %dynamic-update-slic, ...), channel_id=1, replica_groups=mesh['section'=4,'dp'=8] {'dp'}, use_global_device_ids=true, to_apply=%add.32 | all-reduce | flops 7680 | bytes 30720
  44.8 25.3 %all_gather.61 = bf16[1,3072]{1,0:T(2,128)(2,1)S(1)} all-gather(bf16[1,384]{1,0:T(2,128)(2,1)} %param.30), channel_id=1, replica_groups=mesh['section'=4,'dp'=8] {'dp'}, dimensions={1}, use_global_device_ids=true | all-gather | bytes 6912 | tf_op jit(solution)/shard_map/all_gather | solution.py:299
  76.5 3.3 fusion.40
  86.1 31.1 %all-gather.7.cloned.1.call-done = bf16[1,768,768]{2,1,0:T(8,128)(2,1)} async-done(((bf16[1,96,768]{2,1,0:T(8,128)(2,1)}), bf16[1,768,768]{2,1,0:T(8,128)(2,1)}) %all-gather.7.cloned.1.call-update) | async-done | bytes 1179664 | tf_op jit(solution)/shard_map/all_gather | solution.py:294
  119.4 79.2 %all-gather.9.cloned.1.call-done = bf16[1,768,3072]{2,1,0:T(8,128)(2,1)} async-done(((bf16[1,96,3072]{2,1,0:T(8,128)(2,1)}), bf16[1,768,3072]{2,1,0:T(8,128)(2,1)}) %all-gather.9.cloned.1.call-update) | async-done | bytes 4718608 | tf_op jit(solution)/shard_map/all_gather | solution.py:298
  198.6 11.3 multiply_convert_fusion.9
  209.9 68.7 %all-gather.11.cloned.1.call-done = bf16[1,3072,768]{2,1,0:T(8,128)(2,1)} async-done(((bf16[1,384,768]{2,1,0:T(8,128)(2,1)}), bf16[1,3072,768]{2,1,0:T(8,128)(2,1)}) %all-gather.11.cloned.1.call-update) | async-done | bytes 4718608 | tf_op jit(solution)/shard_map/all_gather | solution.py:300
  278.8 4.5 fusion.477
  284.4 4.6 collective-permute-start
  289.7 3.8 collective-permute-done
  309.8 11.6 multiply_convert_fusion.8
  323.9 4.5 collective-permute-start.1
  329.1 3.8 collective-permute-done.1
  350.5 11.5 multiply_convert_fusion.7
  365.5 4.6 collective-permute-start.2
  370.8 3.8 collective-permute-done.2
  375.0 3.2 fusion.43
  383.4 3.2 fusion.363
  394.7 11.5 multiply_convert_fusion.6
  408.7 4.8 collective-permute-start.3
  414.2 3.6 collective-permute-done.3
  425.4 3.2 fusion.367
  438.3 10.9 multiply_convert_fusion.5
  449.3 3.5 convert_reduce_fusion.4
  460.4 3.4 multiply_reduce_fusion.4
  477.2 7.5 collective-permute-done.4
  485.6 3.6 convert_reduce_fusion.3
  497.5 3.4 multiply_reduce_fusion.3
  519.2 3.7 fusion.330
  524.7 6.2 convert_reduce_fusion.2
  539.9 3.3 multiply_reduce_fusion.2
  566.6 3.7 fusion.318
  572.1 6.2 convert_reduce_fusion.1
  585.7 3.3 multiply_reduce_fusion.1
  609.0 3.6 fusion.312
  613.9 5.6 convert_reduce_fusion
  626.0 3.3 multiply_reduce_fusion
  642.4 4.2 fusion.275
  661.9 6.0 add_bitcast_fusion.3
  671.9 4.2 fusion.295
  676.1 4.2 fusion.294
  680.3 10.9 add_bitcast_fusion.2
  692.4 6.8 fusion.333
  699.2 5.8 fusion.327
  705.0 6.0 fusion.321
  711.0 5.9 fusion.315
  716.9 17.5 add_bitcast_fusion
  735.6 6.8 fusion.431
  742.4 5.1 fusion.434
  747.6 6.0 fusion.437
  753.6 5.2 fusion.440
  758.8 17.2 add_bitcast_fusion.1
  778.6 3.9 fusion.216
  789.8 35.3 %reduce-scatter.50.cloned.1.call-done = f32[96,1]{1,0:T(8,128)} async-done(((f32[768,1]{1,0:T(8,128)}), f32[96,1]{1,0:T(8,128)}) %reduce-scatter.50.cloned.1.call-update) | async-done | bytes 400
  826.5 62.3 %reduce-scatter.48.cloned.1.call-done = f32[96,1]{1,0:T(8,128)} async-done(((f32[768,1]{1,0:T(8,128)}), f32[96,1]{1,0:T(8,128)}) %reduce-scatter.48.cloned.1.call-update) | async-done | bytes 400
  890.2 62.3 %reduce-scatter.46.cloned.1.call-done = f32[96,1]{1,0:T(8,128)} async-done(((f32[768,1]{1,0:T(8,128)}), f32[96,1]{1,0:T(8,128)}) %reduce-scatter.46.cloned.1.call-update) | async-done | bytes 400
  953.9 62.1 %reduce-scatter.42.cloned.1.call-done = f32[96,1]{1,0:T(8,128)} async-done(((f32[768,1]{1,0:T(8,128)}), f32[96,1]{1,0:T(8,128)}) %reduce-scatter.42.cloned.1.call-update) | async-done | bytes 400
  1017.3 62.3 %reduce-scatter.40.cloned.1.call-done = f32[96,1]{1,0:T(8,128)} async-done(((f32[768,1]{1,0:T(8,128)}), f32[96,1]{1,0:T(8,128)}) %reduce-scatter.40.cloned.1.call-update) | async-done | bytes 400
  1081.0 65.2 %reduce-scatter.44.cloned.1.call-done = f32[288,1]{1,0:T(8,128)} async-done(((f32[2304,1]{1,0:T(8,128)}), f32[288,1]{1,0:T(8,128)}) %reduce-scatter.44.cloned.1.call-update) | async-done | bytes 1168
  1147.8 65.9 %reduce-scatter.52.cloned.1.call-done = f32[384,1]{1,0:T(8,128)} async-done(((f32[3072,1]{1,0:T(8,128)}), f32[384,1]{1,0:T(8,128)}) %reduce-scatter.52.cloned.1.call-update) | async-done | bytes 1552
  1215.3 70.8 %reduce-scatter.34.cloned.1.call-done = f32[1,96,768]{2,1,0:T(8,128)} async-done(((f32[1,768,768]{2,1,0:T(8,128)}), f32[1,96,768]{2,1,0:T(8,128)}) %reduce-scatter.34.cloned.1.call-update) | async-done | bytes 294928 | tf_op jit(solution)/shard_map/reduce_scatter | solution.py:396
  1286.1 134.1 %reduce-scatter.32.cloned.1.call-done = f32[1,96,2304]{2,1,0:T(8,128)} async-done(((f32[1,768,2304]{2,1,0:T(8,128)}), f32[1,96,2304]{2,1,0:T(8,128)}) %reduce-scatter.32.cloned.1.call-update) | async-done | bytes 884752 | tf_op jit(solution)/shard_map/reduce_scatter | solution.py:394
  1420.3 166.7 %reduce-scatter.38.cloned.1.call-done = f32[1,384,768]{2,1,0:T(8,128)} async-done(((f32[1,3072,768]{2,1,0:T(8,128)}), f32[1,384,768]{2,1,0:T(8,128)}) %reduce-scatter.38.cloned.1.call-update) | async-done | bytes 1179664 | tf_op jit(solution)/shard_map/reduce_scatter | solution.py:402
  1586.9 166.6 %reduce-scatter.36.cloned.1.call-done = f32[1,96,3072]{2,1,0:T(8,128)} async-done(((f32[1,768,3072]{2,1,0:T(8,128)}), f32[1,96,3072]{2,1,0:T(8,128)}) %reduce-scatter.36.cloned.1.call-update) | async-done | bytes 1179664 | tf_op jit(solution)/shard_map/reduce_scatter | solution.py:400
  (1003 shorter events, 272.7 us)
Async XLA Ops:
  7.2 69.3 %all-gather.5.cloned.1.call-start = ((), (), s32[]{:S(2)}) async-start(), calls=%async_computation.13 | async-start | bytes 3981312 | tf_op jit(solution)/shard_map/all_gather | solution.py:292
  7.9 109.3 %all-gather.7.cloned.1.call-start = ((), (), s32[]{:S(2)}) async-start(), calls=%async_computation.14 | async-start | bytes 1327104 | tf_op jit(solution)/shard_map/all_gather | solution.py:294
  8.7 189.9 %all-gather.9.cloned.1.call-start = ((), (), s32[]{:S(2)}) async-start(), calls=%async_computation.15 | async-start | bytes 5308416 | tf_op jit(solution)/shard_map/all_gather | solution.py:298
  9.4 269.3 %all-gather.11.cloned.1.call-start = ((), (), s32[]{:S(2)}) async-start(), calls=%async_computation.16 | async-start | bytes 5308416 | tf_op jit(solution)/shard_map/all_gather | solution.py:300
  10.0 777.0 %reduce-scatter.56.cloned.1.call-start = ((), (), s32[]{:S(2)}) async-start(), calls=%async_computation.29 | async-start | bytes 442368
  44.6 373.6 %copy-start.154 = (f32[768]{0:T(1024)}, f32[768]{0:T(1024)S(1)}, u32[]{:S(2)}) copy-start(f32[768]{0:T(1024)S(1)} %convert_element_type.986) | copy-start | bytes 9220
  44.8 393.5 %copy-start.156 = (f32[768]{0:T(1024)}, f32[768]{0:T(1024)S(1)}, u32[]{:S(2)}) copy-start(f32[768]{0:T(1024)S(1)} %convert_element_type.990) | copy-start | bytes 9220
  72.1 206.7 %copy-start.244 = (f32[1,256]{1,0:T(1,128)}, f32[1,256]{1,0:T(1,128)S(1)}, u32[]{:S(2)}) copy-start(f32[1,256]{1,0:T(1,128)S(1)} %get-tuple-element.191) | copy-start | bytes 3076
  73.5 226.0 %copy-start.228 = (f32[1,256]{1,0:T(1,128)}, f32[1,256]{1,0:T(1,128)S(1)}, u32[]{:S(2)}) copy-start(f32[1,256]{1,0:T(1,128)S(1)} %get-tuple-element.194) | copy-start | bytes 3076
  76.5 223.1 %copy-start.234 = (f32[1,256]{1,0:T(1,128)}, f32[1,256]{1,0:T(1,128)S(1)}, u32[]{:S(2)}) copy-start(f32[1,256]{1,0:T(1,128)S(1)} %get-tuple-element.261) | copy-start | bytes 3076
  83.5 33.7 %copy-start.17 = (bf16[2,256,768]{2,1,0:T(8,128)(2,1)S(1)}, bf16[2,256,768]{2,1,0:T(8,128)(2,1)}, u32[]{:S(2)}) copy-start(bf16[2,256,768]{2,1,0:T(8,128)(2,1)} %param.17) | copy-start | bytes 2359300
  84.3 34.8 %copy-start.202 = (f32[12,256]{1,0:T(8,128)}, f32[12,256]{1,0:T(8,128)S(1)}, u32[]{:S(2)}) copy-start(f32[12,256]{1,0:T(8,128)S(1)} %log_add_fusion.4) | copy-start | bytes 36868
  86.1 112.5 %copy-start.196 = (bf16[12,64,256]{2,1,0:T(8,128)(2,1)}, bf16[12,64,256]{2,1,0:T(8,128)(2,1)S(1)}, u32[]{:S(2)}) copy-start(bf16[12,64,256]{2,1,0:T(8,128)(2,1)S(1)} %convolution_convert_fusion.14) | copy-start | bytes 1179652
  119.1 159.7 %copy-start.64 = (f32[1,256,768]{2,1,0:T(8,128)}, f32[1,256,768]{2,1,0:T(8,128)S(1)}, u32[]{:S(2)}) copy-start(f32[1,256,768]{2,1,0:T(8,128)S(1)} %get-tuple-element.203) | copy-start | bytes 2359300
  119.1 90.8 %copy-start.230 = (f32[256]{0:T(256)}, f32[256]{0:T(256)S(1)}, u32[]{:S(2)}) copy-start(f32[256]{0:T(256)S(1)} %broadcast_multiply_fusion.8) | copy-start | bytes 3076
  119.3 90.6 %copy-start.263 = (f32[256]{0:T(256)}, f32[256]{0:T(256)S(1)}, u32[]{:S(2)}) copy-start(f32[256]{0:T(256)S(1)} %multiply_reduce_fusion.9) | copy-start | bytes 3076
  119.4 90.6 %copy-start.258 = (f32[256]{0:T(256)}, f32[256]{0:T(256)S(1)}, u32[]{:S(2)}) copy-start(f32[256]{0:T(256)S(1)} %fusion.382) | copy-start | bytes 3076
  209.9 73.4 %copy-start.126 = (bf16[256,3072]{1,0:T(8,128)(2,1)}, bf16[256,3072]{1,0:T(8,128)(2,1)S(1)}, u32[]{:S(2)}) copy-start(bf16[256,3072]{1,0:T(8,128)(2,1)S(1)} %get-tuple-element.109) | copy-start | bytes 4718596
  284.4 9.1 collective-permute-start
  289.7 15.3 copy-start.285
  293.7 14.3 copy-start.13
  308.0 13.4 slice-start
  323.9 9.0 collective-permute-start.1
  329.0 16.2 copy-start.287
  332.9 15.3 copy-start.11
  348.2 13.9 slice-start.2
  365.5 9.1 collective-permute-start.2
  392.9 13.3 copy-start.199
  392.9 13.3 slice-start.4
  394.4 97.0 %copy-start.222 = (f32[256]{0:T(256)}, f32[256]{0:T(256)S(1)}, u32[]{:S(2)}) copy-start(f32[256]{0:T(256)S(1)} %broadcast_multiply_fusion.2) | copy-start | bytes 3076
  394.7 96.8 %copy-start.250 = (f32[256]{0:T(256)}, f32[256]{0:T(256)S(1)}, u32[]{:S(2)}) copy-start(f32[256]{0:T(256)S(1)} %fusion.388) | copy-start | bytes 3076
  408.7 12.8 copy-start.81
  408.7 9.1 collective-permute-start.3
  433.0 16.2 slice-start.6
  433.0 19.7 %slice-start.10 = ((s8[4718592]{0:T(1024)(128)(4,1)}), s8[4194304]{0:T(1024)(128)(4,1)S(1)}, s32[]{:S(2)}) async-start(s8[4718592]{0:T(1024)(128)(4,1)} %bitcast.948), calls=%async_computation.40 | async-start | bytes 8388608
  438.0 16.9 copy-start.62
  438.0 16.9 copy-start.224
  438.3 16.7 copy-start.252
  438.3 14.4 slice-start.11
  470.9 14.7 slice-start.8
  470.9 14.6 slice-start.9
  470.9 14.6 copy-start.303
  472.2 13.4 copy-start.302
  472.2 17.0 slice-start.12
  474.5 10.2 collective-permute-start.4
  485.6 24.3 %copy-start.67 = (bf16[1,256,768]{2,1,0:T(8,128)(2,1)}, bf16[1,256,768]{2,1,0:T(8,128)(2,1)S(1)}, u32[]{:S(2)}) copy-start(bf16[1,256,768]{2,1,0:T(8,128)(2,1)S(1)} %get-tuple-element.56) | copy-start | bytes 1179652
  511.6 11.3 collective-permute-start.5
  517.4 13.5 slice-start.14
  555.7 14.6 collective-permute-start.6
  564.8 13.5 slice-start.16
  599.7 12.8 collective-permute-start.7
  639.5 148.9 %reduce-scatter.54.cloned.1.call-start = ((), (), s32[]{:S(2)}) async-start(), calls=%async_computation.28 | async-start | bytes 442368
  641.0 16.0 copy-start.83
  648.9 176.2 %reduce-scatter.50.cloned.1.call-start = ((), (), s32[]{:S(2)}) async-start(), calls=%async_computation.26 | async-start | bytes 442368
  649.9 238.9 %reduce-scatter.48.cloned.1.call-start = ((), (), s32[]{:S(2)}) async-start(), calls=%async_computation.25 | async-start | bytes 442368
  651.0 301.5 %reduce-scatter.46.cloned.1.call-start = ((), (), s32[]{:S(2)}) async-start(), calls=%async_computation.24 | async-start | bytes 442368
  654.9 361.1 %reduce-scatter.42.cloned.1.call-start = ((), (), s32[]{:S(2)}) async-start(), calls=%async_computation.22 | async-start | bytes 442368
  655.9 423.7 %reduce-scatter.40.cloned.1.call-start = ((), (), s32[]{:S(2)}) async-start(), calls=%async_computation.21 | async-start | bytes 442368
  656.9 489.3 %reduce-scatter.44.cloned.1.call-start = ((), (), s32[]{:S(2)}) async-start(), calls=%async_computation.23 | async-start | bytes 1327104
  660.0 553.8 %reduce-scatter.52.cloned.1.call-start = ((), (), s32[]{:S(2)}) async-start(), calls=%async_computation.27 | async-start | bytes 1769472
  661.8 624.3 %reduce-scatter.34.cloned.1.call-start = ((), (), s32[]{:S(2)}) async-start(), calls=%async_computation.18 | async-start | bytes 2654208 | tf_op jit(solution)/shard_map/reduce_scatter | solution.py:396
  667.9 752.3 %reduce-scatter.32.cloned.1.call-start = ((), (), s32[]{:S(2)}) async-start(), calls=%async_computation.17 | async-start | bytes 7962624 | tf_op jit(solution)/shard_map/reduce_scatter | solution.py:394
  691.2 895.7 %reduce-scatter.38.cloned.1.call-start = ((), (), s32[]{:S(2)}) async-start(), calls=%async_computation.20 | async-start | bytes 10616832 | tf_op jit(solution)/shard_map/reduce_scatter | solution.py:402
  734.5 1019.1 %reduce-scatter.36.cloned.1.call-start = ((), (), s32[]{:S(2)}) async-start(), calls=%async_computation.19 | async-start | bytes 10616832 | tf_op jit(solution)/shard_map/reduce_scatter | solution.py:400
  (285 other events, 1139.8 us)
Sparse Core Ops, SparseCore 0:
  10.2 65.6 all-gather.4
  78.1 39.0 all-gather.6
  119.4 79.1 all-gather.8
  200.6 78.0 all-gather.10
  639.7 58.2 reduce-scatter.55
  701.1 60.3 reduce-scatter.53
  764.7 60.3 reduce-scatter.49
  828.4 60.3 reduce-scatter.47
  892.1 60.3 reduce-scatter.45
  955.6 60.3 reduce-scatter.41
  1019.2 60.3 reduce-scatter.39
  1082.9 63.3 reduce-scatter.43
  1149.6 64.0 reduce-scatter.51
  1218.1 68.0 reduce-scatter.33
  1290.7 129.5 reduce-scatter.31
  1424.3 162.5 reduce-scatter.37
  1591.0 162.5 reduce-scatter.35
where the time goes:
time: 1770 us; the launch traced here: 1760 us
  waiting for transfers between devices  1160 us (66%)
  matrix products  312 us (18%)
  other arithmetic  103 us (6%)
  local copies, waits for them, and re-layouts  87.4 us (5%)
  blocking collectives  50.5 us (3%)
  starting transfers between devices  28.9 us (2%)
  between operations  20.6 us (1%)
    unnamed x26, waiting for transfers between devices  418 us
    reduce_scatter x1, waiting for transfers between devices, local(): lax.psum_scatter(totals[10][None], 'dp', scatter_dimension=1, tiled=True)  167 us
    reduce_scatter x1, waiting for transfers between devices, local(): lax.psum_scatter(totals[8][None], 'dp', scatter_dimension=1, tiled=True)  167 us
    reduce_scatter x1, waiting for transfers between devices, local(): lax.psum_scatter(totals[2][None], 'dp', scatter_dimension=1, tiled=True)  134 us
    all_gather x1, waiting for transfers between devices, local(): lax.all_gather(up_matrix, 'dp', axis=1, tiled=True)  79.2 us
    reduce_scatter x1, waiting for transfers between devices, local(): lax.psum_scatter(totals[4][None], 'dp', scatter_dimension=1, tiled=True)  70.8 us
    all_gather x1, waiting for transfers between devices, local(): lax.all_gather(down_matrix, 'dp', axis=1, tiled=True)  68.7 us
    dot_general x5, matrix products, forward_block(): jnp.dot(normed_two, up_matrix, preferred_element_type=jnp.float32)  56.9 us
  transfers between devices with their start and end apart: 25, of which 19 were waited for; matrix products, arithmetic and copies ran while one was open for 13% of the time, Pallas kernels for 0%

commit v1 on v0

--- a/solution.py
+++ b/solution.py
@@ -1,24 +1,391 @@
+import functools
+
 import jax
 import jax.numpy as jnp
 from jax import lax
+from jax.experimental import pallas as pl
+from jax.experimental.pallas import tpu as pltpu
 from jax.sharding import PartitionSpec as P
 
 D = 768
 H = 12
 HD = 64
 GRID = 16
-MICRO = 2
-IMG_MB = 1
-
-
 EPSILON = 1e-06
 MASKED = -1e30
-
-
-def shifted(value, axis, steps):
-    count = lax.axis_size(axis)
-    first, last = (max(0, -steps), min(count, count - steps))
-    return lax.ppermute(value, axis, [(source, source + steps) for source in range(first, last)])
+GROUPS = 8
+LANES = 128
+MESH = pl.DeviceIdType.MESH
+
+
+def place(replicas):
+    section = lax.axis_index("section")
+    dp = lax.axis_index("dp")
+    x, core = lax.div(section, 2), lax.rem(section, 2)
+    group, m = lax.div(dp, replicas), lax.rem(dp, replicas)
+    z, y = lax.div(group, 2), lax.rem(group, 2)
+    return x, core, z, y, m
+
+
+def device(replicas, x, core, z, y, m):
+    return (2 * x + core, (2 * z + y) * replicas + m)
+
+
+def next_pairs(sections, dp_size, step):
+    replicas = dp_size // GROUPS
+    pairs = []
+    for section in range(sections):
+        for dp in range(dp_size):
+            x, core = divmod(section, 2)
+            group, m = divmod(dp, replicas)
+            z, y = divmod(group, 2)
+            role = 2 * x + z % 2 + step
+            if 0 <= role < sections:
+                to = device(replicas, role // 2, core, z - z % 2 + role % 2, y, m)
+                pairs.append((section * dp_size + dp, to[0] * dp_size + to[1]))
+    return pairs
+
+
+def enter(replicas):
+    x, core, z, y, m = place(replicas)
+    odd = lax.rem(z, 2)
+    barrier = pltpu.get_barrier_semaphore()
+
+    def greet(to):
+        pl.semaphore_signal(barrier, inc=1, device_id=to, device_id_type=MESH)
+
+    greet(device(replicas, x, 1 - core, z, y, m))
+    greet(device(replicas, x, core, z, 1 - y, m))
+    for k in range(2):
+
+        @pl.when(jnp.logical_or(core != odd, lax.div(z, 2) != k))
+        def _():
+            greet(device(replicas, x, odd, core + 2 * k, y, m))
+
+    pl.semaphore_wait(barrier, 4 - jnp.where(core == odd, 1, 0))
+
+
+def remote(source, target, send, arrive, to):
+    return pltpu.make_async_remote_copy(
+        src_ref=source,
+        dst_ref=target,
+        send_sem=send,
+        recv_sem=arrive,
+        device_id=to,
+        device_id_type=MESH,
+    )
+
+
+def swap_start(replicas, sources, targets, send, arrive):
+    x, core, z, y, m = place(replicas)
+    odd = lax.rem(z, 2)
+    to = device(replicas, x, odd, z - odd + core, y, m)
+    for n, (source, target) in enumerate(zip(sources, targets)):
+
+        @pl.when(core == odd)
+        def _():
+            pltpu.make_async_copy(source, target, arrive.at[n]).start()
+
+        @pl.when(core != odd)
+        def _():
+            remote(source, target, send.at[n], arrive.at[n], to).start()
+
+
+def swap_wait(replicas, sources, targets, send, arrive):
+    x, core, z, y, m = place(replicas)
+    odd = lax.rem(z, 2)
+    to = device(replicas, x, odd, z - odd + core, y, m)
+    for n, (source, target) in enumerate(zip(sources, targets)):
+
+        @pl.when(core == odd)
+        def _():
+            pltpu.make_async_copy(source, target, arrive.at[n]).wait()
+
+        @pl.when(core != odd)
+        def _():
+            copy = remote(source, target, send.at[n], arrive.at[n], to)
+            copy.wait_recv()
+            copy.wait_send()
+
+
+def gather_kernel(replicas, count, swaps, *refs):
+    parts, refs = refs[:count], refs[count:]
+    swap_in, refs = refs[:swaps], refs[swaps:]
+    wholes, refs = refs[:count], refs[count:]
+    swap_out, refs = refs[:swaps], refs[swaps:]
+    send, arrive, swap_send, swap_arrive = refs
+    x, core, z, y, m = place(replicas)
+    odd = lax.rem(z, 2)
+    half = lax.div(z, 2)
+    mine = 2 * z + y
+    sibling = device(replicas, x, 1 - core, z, y, m)
+    across = device(replicas, x, core, z, 1 - y, m)
+    enter(replicas)
+    swap_start(replicas, swap_in, swap_out, swap_send, swap_arrive)
+
+    def along(n, k):
+        return remote(
+            parts[n],
+            wholes[n].at[mine],
+            send.at[n, k],
+            arrive.at[n, mine],
+            device(replicas, x, odd, core + 2 * k, y, m),
+        )
+
+    def own(n):
+        return pltpu.make_async_copy(parts[n], wholes[n].at[mine], arrive.at[n, mine])
+
+    def relay(n, slot, group, to):
+        block = wholes[n].at[group]
+        return remote(block, block, send.at[n, slot], arrive.at[n, group], to)
+
+    for n in range(count):
+        for k in range(2):
+            here = jnp.logical_and(core == odd, half == k)
+
+            @pl.when(here)
+            def _():
+                own(n).start()
+
+            @pl.when(jnp.logical_not(here))
+            def _():
+                along(n, k).start()
+
+    for n in range(count):
+        for k in range(2):
+            here = jnp.logical_and(core == odd, half == k)
+            group = 2 * (core + 2 * k) + y
+
+            @pl.when(here)
+            def _():
+                own(n).wait()
+
+            @pl.when(jnp.logical_not(here))
+            def _():
+                relay(n, 2 + k, group, sibling).wait_recv()
+
+            relay(n, 4 + k, group, across).start()
+            relay(n, 2 + k, group, sibling).start()
+        for k in range(2):
+            group = 2 * (core + 2 * k) + 1 - y
+            relay(n, 6 + k, group, sibling).wait_recv()
+            relay(n, 6 + k, group, sibling).start()
+    for n in range(count):
+        for k in range(2):
+            for row in range(2):
+                group = 2 * (1 - core + 2 * k) + row
+                relay(n, 2 + k, group, sibling).wait_recv()
+    for n in range(count):
+        for k in range(2):
+            here = jnp.logical_and(core == odd, half == k)
+            group = 2 * (core + 2 * k) + y
+            other = 2 * (core + 2 * k) + 1 - y
+
+            @pl.when(jnp.logical_not(here))
+            def _():
+                along(n, k).wait_send()
+
+            relay(n, 2 + k, group, sibling).wait_send()
+            relay(n, 4 + k, group, across).wait_send()
+            relay(n, 6 + k, other, sibling).wait_send()
+    swap_wait(replicas, swap_in, swap_out, swap_send, swap_arrive)
+
+
+def gather(replicas, parts, swaps):
+    anywhere = pl.BlockSpec(memory_space=pl.ANY)
+    count, extra = len(parts), len(swaps)
+    outs = [jax.ShapeDtypeStruct((GROUPS, *part.shape), part.dtype) for part in parts]
+    outs += [jax.ShapeDtypeStruct(value.shape, value.dtype) for value in swaps]
+    results = pl.pallas_call(
+        functools.partial(gather_kernel, replicas, count, extra),
+        out_shape=outs,
+        in_specs=[anywhere] * (count + extra),
+        out_specs=[anywhere] * (count + extra),
+        scratch_shapes=[
+            pltpu.SemaphoreType.DMA((count, 8)),
+            pltpu.SemaphoreType.DMA((count, GROUPS)),
+            pltpu.SemaphoreType.DMA((extra,)),
+            pltpu.SemaphoreType.DMA((extra,)),
+        ],
+        compiler_params=pltpu.CompilerParams(collective_id=0, has_side_effects=True),
+        name="gather",
+    )(*parts, *swaps)
+    return results[:count], results[count:]
+
+
+def rows_of(dtype):
+    return 16 if dtype == jnp.bfloat16 else 8
+
+
+def reduce_kernel(replicas, count, swaps, *refs):
+    parts, refs = refs[:count], refs[count:]
+    swap_in, refs = refs[:swaps], refs[swaps:]
+    outs, refs = refs[:count], refs[count:]
+    swap_out, refs = refs[:swaps], refs[swaps:]
+    held, refs = refs[:count], refs[count:]
+    first, refs = refs[:count], refs[count:]
+    second, refs = refs[:count], refs[count:]
+    third, refs = refs[:count], refs[count:]
+    send, load, arrive, swap_send, swap_arrive = refs
+    x, core, z, y, m = place(replicas)
+    odd = lax.rem(z, 2)
+    half = lax.div(z, 2)
+    sibling = device(replicas, x, 1 - core, z, y, m)
+    across = device(replicas, x, core, z, 1 - y, m)
+    enter(replicas)
+    swap_start(replicas, swap_in, swap_out, swap_send, swap_arrive)
+
+    def to_sibling(n, slot):
+        k, other = slot % 2, slot < 2
+        group = 2 * (1 - core + 2 * k) + (1 - y if other else y)
+        return remote(
+            parts[n].at[group], first[n].at[slot], send.at[n, slot], arrive.at[n, slot], sibling
+        )
+
+    def loading(n, slot):
+        k, other = slot % 2, slot < 2
+        group = 2 * (core + 2 * k) + (1 - y if other else y)
+        return pltpu.make_async_copy(parts[n].at[group], held[n].at[slot], load.at[n, slot])
+
+    def to_across(n, k):
+        return remote(
+            held[n].at[k], second[n].at[k], send.at[n, 4 + k], arrive.at[n, 4 + k], across
+        )
+
+    def to_owner(n, k):
+        return remote(
+            held[n].at[2 + k],
+            third[n].at[half],
+            send.at[n, 6 + k],
+            arrive.at[n, 6 + half],
+            device(replicas, x, odd, core + 2 * k, y, m),
+        )
+
+    def from_other(n, k):
+        return remote(
+            held[n].at[2 + k],
+            third[n].at[k],
+            send.at[n, 6 + k],
+            arrive.at[n, 6 + k],
+            device(replicas, x, odd, core + 2 * k, y, m),
+        )
+
+    def add(n, slot, source, index):
+        step = rows_of(held[n].dtype)
+        count_rows = held[n].shape[1] // step
+
+        def body(i, carry):
+            rows = pl.ds(pl.multiple_of(i * step, step), step)
+            total = held[n][slot, rows, :].astype(jnp.float32) + source[index, rows, :].astype(
+                jnp.float32
+            )
+            held[n][slot, rows, :] = total.astype(held[n].dtype)
+            return carry
+
+        lax.fori_loop(0, count_rows, body, 0)
+
+    for n in range(count):
+        for slot in range(4):
+            to_sibling(n, slot).start()
+        for slot in range(4):
+            loading(n, slot).start()
+
+    for n in range(count):
+        for k in range(2):
+            loading(n, k).wait()
+            to_sibling(n, k).wait_recv()
+            add(n, k, first[n], k)
+            to_across(n, k).start()
+        for k in range(2):
+            loading(n, 2 + k).wait()
+            to_sibling(n, 2 + k).wait_recv()
+            add(n, 2 + k, first[n], 2 + k)
+        for k in range(2):
+            here = jnp.logical_and(core == odd, half == k)
+            to_across(n, k).wait_recv()
+            add(n, 2 + k, second[n], k)
+
+            @pl.when(jnp.logical_not(here))
+            def _():
+                to_owner(n, k).start()
+
+    for n in range(count):
+        step = rows_of(held[n].dtype)
+        count_rows = held[n].shape[1] // step
+        for k in range(2):
+            here = jnp.logical_and(core == odd, half == k)
+
+            @pl.when(jnp.logical_not(here))
+            def _():
+                from_other(n, k).wait_recv()
+
+        def total(pick):
+            def body(i, carry):
+                rows = pl.ds(pl.multiple_of(i * step, step), step)
+                low, high = pick(rows)
+                outs[n][rows, :] = low.astype(jnp.float32) + high.astype(jnp.float32)
+                return carry
+
+            lax.fori_loop(0, count_rows, body, 0)
+
+        @pl.when(core != odd)
+        def _():
+            total(lambda rows: (third[n][0, rows, :], third[n][1, rows, :]))
+
+        @pl.when(jnp.logical_and(core == odd, half == 0))
+        def _():
+            total(lambda rows: (held[n][2, rows, :], third[n][1, rows, :]))
+
+        @pl.when(jnp.logical_and(core == odd, half == 1))
+        def _():
+            total(lambda rows: (third[n][0, rows, :], held[n][3, rows, :]))
+
+    for n in range(count):
+        for slot in range(4):
+            to_sibling(n, slot).wait_send()
+        for k in range(2):
+            here = jnp.logical_and(core == odd, half == k)
+            to_across(n, k).wait_send()
+
+            @pl.when(jnp.logical_not(here))
+            def _():
+                to_owner(n, k).wait_send()
+
+    swap_wait(replicas, swap_in, swap_out, swap_send, swap_arrive)
+
+
+def reduce(replicas, parts, swaps):
+    anywhere = pl.BlockSpec(memory_space=pl.ANY)
+    count, extra = len(parts), len(swaps)
+    blocks = [part.shape[1:] for part in parts]
+    outs = [jax.ShapeDtypeStruct(block, jnp.float32) for block in blocks]
+    outs += [jax.ShapeDtypeStruct(value.shape, value.dtype) for value in swaps]
+
+    def buffers(slots):
+        return [pltpu.VMEM((slots, *part.shape[1:]), part.dtype) for part in parts]
+
+    results = pl.pallas_call(
+        functools.partial(reduce_kernel, replicas, count, extra),
+        out_shape=outs,
+        in_specs=[anywhere] * (count + extra),
+        out_specs=[pl.BlockSpec(memory_space=pltpu.VMEM)] * count + [anywhere] * extra,
+        scratch_shapes=buffers(4)
+        + buffers(4)
+        + buffers(2)
+        + buffers(2)
+        + [
+            pltpu.SemaphoreType.DMA((count, 8)),
+            pltpu.SemaphoreType.DMA((count, 4)),
+            pltpu.SemaphoreType.DMA((count, 8)),
+            pltpu.SemaphoreType.DMA((extra,)),
+            pltpu.SemaphoreType.DMA((extra,)),
+        ],
+        compiler_params=pltpu.CompilerParams(
+            collective_id=1, has_side_effects=True, vmem_limit_bytes=56 * 1024 * 1024
+        ),
+        name="reduce",
+    )(*parts, *swaps)
+    return results[:count], results[count:]
 
 
 def layer_norm(values, gain_vector, shift_vector):
@@ -265,161 +632,126 @@
     return (grad_input, grads)
 
 
-def local(
-    images,
-    cotangent,
-    kept_count,
-    kept_index,
-    gain_one,
-    shift_one,
-    qkv_matrix,
-    qkv_shift,
-    proj_matrix,
-    proj_shift,
-    gain_two,
-    shift_two,
-    up_matrix,
-    up_shift,
-    down_matrix,
-    down_shift,
-    frequency,
-):
+def rows_from(vector):
+    short = -vector.shape[0] % LANES
+    return jnp.pad(vector, (0, short)).reshape(-1, LANES)
+
+
+def pack(vectors):
+    block = jnp.concatenate([rows_from(vector) for vector in vectors], axis=0)
+    return jnp.pad(block, ((0, -block.shape[0] % 16), (0, 0)))
+
+
+def unpack(block, sizes):
+    found, start = [], 0
+    for size in sizes:
+        count = -(-size // LANES)
+        flat = block[:, start : start + count].reshape(block.shape[0], count * LANES)
+        found.append(flat[:, :size])
+        start += count
+    return found
+
+
+MATRICES = (2, 4, 8, 10)
+VECTORS = (0, 1, 3, 5, 6, 7, 9, 11, 12)
+
+
+def local(images, cotangent, kept_count, kept_index, *weights):
     sections = lax.axis_size("section")
-    section_no = lax.axis_index("section")
-    gathered = (
-        lax.all_gather(gain_one, "dp", axis=1, tiled=True),
-        lax.all_gather(shift_one, "dp", axis=1, tiled=True),
-        lax.all_gather(qkv_matrix, "dp", axis=1, tiled=True),
-        lax.all_gather(qkv_shift, "dp", axis=1, tiled=True),
-        lax.all_gather(proj_matrix, "dp", axis=1, tiled=True),
-        lax.all_gather(proj_shift, "dp", axis=1, tiled=True),
-        lax.all_gather(gain_two, "dp", axis=1, tiled=True),
-        lax.all_gather(shift_two, "dp", axis=1, tiled=True),
-        lax.all_gather(up_matrix, "dp", axis=1, tiled=True),
-        lax.all_gather(up_shift, "dp", axis=1, tiled=True),
-        lax.all_gather(down_matrix, "dp", axis=1, tiled=True),
-        lax.all_gather(down_shift, "dp", axis=1, tiled=True),
-        lax.all_gather(frequency, "dp", axis=1, tiled=True),
-    )
-    params = tuple((values[0] for values in gathered))
-    shard_shapes = tuple(
-        (
-            values.shape
-            for values in (
-                gain_one,
-                shift_one,
-                qkv_matrix,
-                qkv_shift,
-                proj_matrix,
-                proj_shift,
-                gain_two,
-                shift_two,
-                up_matrix,
-                up_shift,
-                down_matrix,
-                down_shift,
-                frequency,
-            )
-        )
-    )
-    patches = images.shape[1]
-    keep_all = (jnp.arange(patches)[None, :] < kept_count[:, None]).astype(jnp.float32)
-    total_steps = MICRO + sections - 1
-    incoming = jnp.zeros((IMG_MB, patches, D), jnp.bfloat16)
-    outputs = jnp.zeros((MICRO * IMG_MB, patches, D), jnp.float32)
+    dp_size = lax.axis_size("dp")
+    replicas = dp_size // GROUPS
+    x, core, z, y, m = place(replicas)
+    role = 2 * x + lax.rem(z, 2)
+    subgroups = [[g * replicas + r for r in range(replicas)] for g in range(GROUPS)]
+    if replicas > 1:
+        weights = tuple(
+            lax.all_gather(value, "dp", axis=1, tiled=True, axis_index_groups=subgroups)
+            for value in weights
+        )
+    weights = tuple(value[0] for value in weights)
+    sizes = [weights[n].shape[0] for n in VECTORS]
+    per_device, patches = images.shape[:2]
+    keep = (jnp.arange(patches)[None, :] < kept_count[:, None]).astype(jnp.int32)
+    facts = jnp.stack([keep, kept_index], axis=1).astype(jnp.float32)
+    facts = jnp.pad(facts, ((0, 0), (0, 6), (0, 0)))
+
+    parts = [weights[n] for n in MATRICES] + [pack([weights[n] for n in VECTORS])]
+    wholes, swapped = gather(replicas, parts, [images, cotangent, facts])
+    images, cotangent, facts = swapped
+    params = [None] * len(weights)
+    for n, whole in zip(MATRICES, wholes):
+        params[n] = whole.reshape(GROUPS * whole.shape[1], whole.shape[2])
+    for n, vector in zip(VECTORS, unpack(wholes[-1], sizes)):
+        params[n] = vector.reshape(-1)
+    keep_all = facts[:, 0]
+    index_all = facts[:, 1].astype(jnp.int32)
+
+    total_steps = per_device + sections - 1
+    forth = next_pairs(sections, dp_size, 1)
+    back = next_pairs(sections, dp_size, -1)
+    axes = ("section", "dp")
+    incoming = jnp.zeros((1, patches, D), jnp.bfloat16)
+    outputs = jnp.zeros((per_device, patches, D), jnp.float32)
     kept_steps = []
     for moment in range(total_steps):
-        batch_no = moment - section_no
-        valid = (batch_no >= 0) & (batch_no < MICRO)
-        start = jnp.clip(batch_no, 0, MICRO - 1) * IMG_MB
-        if moment < MICRO:
-            fresh = lax.slice_in_dim(images, moment * IMG_MB, (moment + 1) * IMG_MB, axis=0)
+        batch_no = moment - role
+        valid = (batch_no >= 0) & (batch_no < per_device)
+        start = jnp.clip(batch_no, 0, per_device - 1)
+        if moment < per_device:
+            fresh = lax.slice_in_dim(images, moment, moment + 1, axis=0)
+            section_in = jnp.where(role == 0, fresh, incoming)
         else:
-            fresh = jnp.zeros((IMG_MB, patches, D), jnp.bfloat16)
-        section_in = jnp.where(section_no == 0, fresh, incoming)
-        keep_rows = lax.dynamic_slice_in_dim(keep_all, start, IMG_MB, 0)
-        index_rows = lax.dynamic_slice_in_dim(kept_index, start, IMG_MB, 0)
+            section_in = incoming
+        keep_rows = lax.dynamic_slice_in_dim(keep_all, start, 1, 0)
+        index_rows = lax.dynamic_slice_in_dim(index_all, start, 1, 0)
         result, saved = forward_block(section_in, keep_rows, index_rows, params)
-        result_low = result.astype(jnp.bfloat16)
-        kept_steps.append((section_in, keep_rows, index_rows))
+        kept_steps.append((saved, keep_rows, index_rows))
         outputs = jnp.where(
             valid, lax.dynamic_update_slice_in_dim(outputs, result, start, 0), outputs
         )
         if moment < total_steps - 1:
-            incoming = shifted(result_low, "section", 1)
-    gathered = (
-        lax.all_gather(gain_one, "dp", axis=1, tiled=True),
-        lax.all_gather(shift_one, "dp", axis=1, tiled=True),
-        lax.all_gather(qkv_matrix, "dp", axis=1, tiled=True),
-        lax.all_gather(qkv_shift, "dp", axis=1, tiled=True),
-        lax.all_gather(proj_matrix, "dp", axis=1, tiled=True),
-        lax.all_gather(proj_shift, "dp", axis=1, tiled=True),
-        lax.all_gather(gain_two, "dp", axis=1, tiled=True),
-        lax.all_gather(shift_two, "dp", axis=1, tiled=True),
-        lax.all_gather(up_matrix, "dp", axis=1, tiled=True),
-        lax.all_gather(up_shift, "dp", axis=1, tiled=True),
-        lax.all_gather(down_matrix, "dp", axis=1, tiled=True),
-        lax.all_gather(down_shift, "dp", axis=1, tiled=True),
-        lax.all_gather(frequency, "dp", axis=1, tiled=True),
-    )
-    params = tuple((values[0] for values in gathered))
-    totals = tuple((jnp.zeros(values.shape, jnp.float32) for values in params))
-    reduced = tuple((jnp.zeros(shape_now, jnp.float32) for shape_now in shard_shapes))
-    incoming = jnp.zeros((IMG_MB, patches, D), jnp.bfloat16)
-    input_grads = jnp.zeros((MICRO * IMG_MB, patches, D), jnp.float32)
+            incoming = lax.ppermute(result.astype(jnp.bfloat16), axes, forth)
+    totals = tuple(jnp.zeros(values.shape, jnp.float32) for values in params)
+    incoming = jnp.zeros((1, patches, D), jnp.bfloat16)
+    input_grads = jnp.zeros((per_device, patches, D), jnp.float32)
     for moment in range(total_steps):
         earlier = total_steps - 1 - moment
-        batch_no = earlier - section_no
-        valid = (batch_no >= 0) & (batch_no < MICRO)
-        start = jnp.clip(batch_no, 0, MICRO - 1) * IMG_MB
+        batch_no = earlier - role
+        valid = (batch_no >= 0) & (batch_no < per_device)
+        start = jnp.clip(batch_no, 0, per_device - 1)
         from_next = jnp.where(
-            section_no == sections - 1,
-            lax.dynamic_slice_in_dim(cotangent, start, IMG_MB, 0),
-            incoming,
+            role == sections - 1, lax.dynamic_slice_in_dim(cotangent, start, 1, 0), incoming
         )
         grad_out = jnp.where(valid, from_next.astype(jnp.float32), 0.0)
-        section_in, keep_rows, index_rows = kept_steps[earlier]
-        saved = forward_block(section_in, keep_rows, index_rows, params)[1]
+        saved, keep_rows, index_rows = kept_steps[earlier]
         grad_input, grads = backward_block(grad_out, keep_rows, index_rows, saved, params)
-        totals = tuple((running + fresh_grad for running, fresh_grad in zip(totals, grads)))
-        grad_low = grad_input.astype(jnp.bfloat16)
+        totals = tuple(running + fresh_grad for running, fresh_grad in zip(totals, grads))
         input_grads = jnp.where(
             valid, lax.dynamic_update_slice_in_dim(input_grads, grad_input, start, 0), input_grads
         )
         if moment < total_steps - 1:
-            incoming = shifted(grad_low, "section", -1)
-    reduced = (
-        lax.psum_scatter(totals[0][None], "dp", scatter_dimension=1, tiled=True),
-        lax.psum_scatter(totals[1][None], "dp", scatter_dimension=1, tiled=True),
-        lax.psum_scatter(totals[2][None], "dp", scatter_dimension=1, tiled=True),
-        lax.psum_scatter(totals[3][None], "dp", scatter_dimension=1, tiled=True),
-        lax.psum_scatter(totals[4][None], "dp", scatter_dimension=1, tiled=True),
-        lax.psum_scatter(totals[5][None], "dp", scatter_dimension=1, tiled=True),
-        lax.psum_scatter(totals[6][None], "dp", scatter_dimension=1, tiled=True),
-        lax.psum_scatter(totals[7][None], "dp", scatter_dimension=1, tiled=True),
-        lax.psum_scatter(totals[8][None], "dp", scatter_dimension=1, tiled=True),
-        lax.psum_scatter(totals[9][None], "dp", scatter_dimension=1, tiled=True),
-        lax.psum_scatter(totals[10][None], "dp", scatter_dimension=1, tiled=True),
-        lax.psum_scatter(totals[11][None], "dp", scatter_dimension=1, tiled=True),
-        lax.psum_scatter(totals[12][None], "dp", scatter_dimension=1, tiled=True),
-    )
-    return (
-        outputs[None],
-        input_grads[None],
-        reduced[0],
-        reduced[1],
-        reduced[2],
-        reduced[3],
-        reduced[4],
-        reduced[5],
-        reduced[6],
-        reduced[7],
-        reduced[8],
-        reduced[9],
-        reduced[10],
-        reduced[11],
-        reduced[12],
-    )
+            incoming = lax.ppermute(grad_input.astype(jnp.bfloat16), axes, back)
+
+    parts = [
+        totals[n].astype(jnp.bfloat16).reshape(GROUPS, -1, totals[n].shape[1]) for n in MATRICES
+    ]
+    vectors = [totals[n].reshape(GROUPS, -1) for n in VECTORS]
+    small = jnp.stack([pack([vector[g] for vector in vectors]) for g in range(GROUPS)])
+    sums, swapped = reduce(replicas, parts[::-1] + [small], [outputs, input_grads])
+    outputs, input_grads = swapped
+    grads = [None] * len(weights)
+    for n, value in zip(MATRICES[::-1], sums):
+        grads[n] = value
+    for n, vector in zip(VECTORS, unpack(sums[-1][None], sizes)):
+        grads[n] = vector[0]
+    if replicas > 1:
+        grads = [
+            lax.psum_scatter(
+                value, "dp", scatter_dimension=0, tiled=True, axis_index_groups=subgroups
+            )
+            for value in grads
+        ]
+    return (outputs[None], input_grads[None], *(value[None] for value in grads))
 
 
 def solution(mesh):

time: 1770 us -> 903 us (0.51)
  waiting for transfers between devices: 1160 us -> 24.8 us
  Pallas kernels: 0 us -> 256 us
  local copies, waits for them, and re-layouts: 87.4 us -> 163 us
  blocking collectives: 50.5 us -> 0 us
    reduce_scatter x4 -> x0, waiting for transfers between devices: 538 us -> none  [the longest x1 167 us: local(): lax.psum_scatter(totals[10][None], 'dp', scatter_dimension=1, tiled=True)]
    unnamed x26 -> x0, waiting for transfers between devices: 418 us -> none
    pallas_call x0 -> x2, Pallas kernels: none -> 256 us  [the longest x1 131 us: gather(): pl.pallas_call(functools.partial(gather_kernel, replicas, count, extra),...]
    all_gather x4 -> x0, waiting for transfers between devices: 179 us -> none  [the longest x1 79.2 us: local(): lax.all_gather(up_matrix, 'dp', axis=1, tiled=True)]
    reshape x0 -> x62, local copies, waits for them, and re-layouts: none -> 62 us  [the longest x61 60.6 us: rows_from(): return jnp.pad(vector, (0, short)).reshape(-1, LANES)]
    all_gather x1 -> x0, blocking collectives: 25.3 us -> none  [local(): lax.all_gather(up_shift, 'dp', axis=1, tiled=True)]
    unnamed x1 -> x0, blocking collectives: 25.2 us -> none
    unnamed x685 -> x864, local copies, waits for them, and re-layouts: 56.2 us -> 37 us
  transfers between devices with their start and end apart: 25 -> 8, of which waited for: 19 -> 4; matrix products, arithmetic and copies ran while one was open for 13% -> 7% of each run, Pallas kernels for 0% -> 0%
where the time goes in v1:
time: 903 us; the launch traced here: 893 us
  matrix products  308 us (34%)
  Pallas kernels  256 us (28%)
  local copies, waits for them, and re-layouts  163 us (18%)
  other arithmetic  111 us (12%)
  waiting for transfers between devices  24.8 us (3%)
  starting transfers between devices  23.5 us (3%)
    pallas_call x1, Pallas kernels, gather(): pl.pallas_call(functools.partial(gather_kernel, replicas, count, extra),...  131 us
    pallas_call x1, Pallas kernels, reduce(): pl.pallas_call(functools.partial(reduce_kernel, replicas, count, extra),...  125 us
    reshape x61, local copies, waits for them, and re-layouts, rows_from(): return jnp.pad(vector, (0, short)).reshape(-1, LANES)  60.6 us
    dot_general x5, matrix products, forward_block(): jnp.dot(normed_two, up_matrix, preferred_element_type=jnp.float32)  57.3 us
    unnamed x864, local copies, waits for them, and re-layouts  37 us
    dot_general x5, matrix products, backward_block(): jnp.einsum('bpd,bpf->df', normed_two, grad_hidden, preferred_element_type...  36.7 us
    dot_general x5, matrix products, backward_block(): jnp.einsum('bpf,bpd->fd', active, grad_two, preferred_element_type=jnp.fl...  36.5 us
    dot_general x5, matrix products, backward_block(): jnp.einsum('bpd,bpe->de', normed, grad_mixed, preferred_element_type=jnp....  34.7 us
  transfers between devices with their start and end apart: 8, of which 4 were waited for; matrix products, arithmetic and copies ran while one was open for 7% of the time, Pallas kernels for 0%

profile of v1, /device:TPU:17, one launch (start us, length us, event | category | flops | bytes accessed | tf_op | source)
XLA Modules:
  0.0 893.2 jit_solution(9379622938998324785)
XLA Ops:
  7.5 130.9 %gather.1 = (bf16[8,96,2304]{2,1,0:T(8,128)(2,1)}, bf16[8,96,768]{2,1,0:T(8,128)(2,1)}, bf16[8,96,3072]{2,1,0:T(8,128)(2,1)}, bf16[8,384,768]{2,1,0:T(8,128)(2,1...) custom-call(bf16[96,2304]{1,0:T(8,128)(2,1)} %bitcast.980, ...), custom_call_target="tpu_custom_call" | custom-call | tf_op jit(solution)/shard_map/gather/pallas_call | solution.py:199
  143.8 3.2 fusion
  150.1 2.3 fusion.229
  156.0 3.1 convolution_convert_fusion.14
  160.9 11.3 %multiply_convert_fusion.9 = (bf16[256,3072]{1,0:T(8,128)(2,1)S(1)}, f32[256,3072]{1,0:T(8,128)}, f32[256,3072]{1,0:T(8,128)}) fusion(f32[3072]{0:T(1024)S(1)} %reshape.3405, bf16[768,3072]{1,0:T(8,128)(2,1)} %bitcast.1080, f32[1,256,768]{2,1,0:T(8,128)S(1)} %get-tuple-element.316, f32[768]{0:T(1024)S(1)} %reshape.3404, f32[768]{0:T(1024)S(1)} %reshape.3403, ...), kind=kOutput, calls=%fused_computation.112 | convolution fusion | flops 1260847104 | bytes 13389824 | tf_op jit(solution)/shard_map/dot_general | solution.py:485
  173.5 4.6 select_dynamic-update-slice_fusion.8
  178.2 4.6 collective-permute-start
  182.8 8.0 collective-permute-done
  191.3 3.2 fusion.1
  204.8 2.9 convolution_convert_fusion.13
  208.6 12.1 %multiply_convert_fusion.8 = (bf16[256,3072]{1,0:T(8,128)(2,1)S(1)}, f32[256,3072]{1,0:T(8,128)}, f32[256,3072]{1,0:T(8,128)}) fusion(f32[3072]{0:T(1024)S(1)} %reshape.3405, bf16[768,3072]{1,0:T(8,128)(2,1)} %bitcast.1081, f32[1,256,768]{2,1,0:T(8,128)S(1)} %get-tuple-element.322, f32[256]{0:T(256)S(1)} %fusion.268, f32[256]{0:T(256)S(1)} %broadcast_multiply_fusion.6, ...), kind=kOutput, calls=%fused_computation.96 | convolution fusion | flops 1260847104 | bytes 13389824 | tf_op jit(solution)/shard_map/dot_general | solution.py:485
  220.8 4.0 select_dynamic-update-slice_fusion.7
  224.8 4.1 collective-permute-start.1
  229.5 6.6 collective-permute-done.1
  242.2 2.8 fusion.237
  249.3 2.9 convolution_convert_fusion.12
  253.7 11.5 %multiply_convert_fusion.7 = (bf16[256,3072]{1,0:T(8,128)(2,1)S(1)}, f32[256,3072]{1,0:T(8,128)}, f32[256,3072]{1,0:T(8,128)}) fusion(f32[3072]{0:T(1024)S(1)} %copy-done.323, bf16[768,3072]{1,0:T(8,128)(2,1)} %bitcast.1082, f32[1,256,768]{2,1,0:T(8,128)S(1)} %get-tuple-element.328, f32[256]{0:T(256)S(1)} %fusion.270, f32[256]{0:T(256)S(1)} %broadcast_multiply_fusion.4, ...), kind=kOutput, calls=%fused_computation.80 | convolution fusion | flops 1260847104 | bytes 13389824 | tf_op jit(solution)/shard_map/dot_general | solution.py:485
  265.4 4.0 select_dynamic-update-slice_fusion.6
  269.4 4.1 collective-permute-start.2
  274.1 5.7 collective-permute-done.2
  293.6 2.9 convolution_convert_fusion.11
  297.5 11.4 %multiply_convert_fusion.6 = (bf16[256,3072]{1,0:T(8,128)(2,1)S(1)}, f32[256,3072]{1,0:T(8,128)}, f32[256,3072]{1,0:T(8,128)}) fusion(f32[3072]{0:T(1024)S(1)} %copy-done.324, bf16[768,3072]{1,0:T(8,128)(2,1)} %bitcast.1083, f32[1,256,768]{2,1,0:T(8,128)S(1)} %get-tuple-element.334, f32[256]{0:T(256)S(1)} %fusion.272, f32[256]{0:T(256)S(1)} %broadcast_multiply_fusion.2, ...), kind=kOutput, calls=%fused_computation.64 | convolution fusion | flops 1260847104 | bytes 13389824 | tf_op jit(solution)/shard_map/dot_general | solution.py:485
  309.0 4.0 select_dynamic-update-slice_fusion.5
  313.0 4.7 collective-permute-start.3
  318.8 4.6 collective-permute-done.3
  330.5 2.9 fusion.245
  338.5 2.9 convolution_convert_fusion.10
  342.4 11.0 %multiply_convert_fusion.5 = (bf16[256,3072]{1,0:T(8,128)(2,1)}, f32[256,3072]{1,0:T(8,128)S(1)}, f32[256,3072]{1,0:T(8,128)S(1)}) fusion(f32[3072]{0:T(1024)S(1)} %copy-done.325, bf16[768,3072]{1,0:T(8,128)(2,1)} %bitcast.1084, f32[1,256,768]{2,1,0:T(8,128)S(1)} %get-tuple-element.340, f32[256]{0:T(256)S(1)} %fusion.274, ...), kind=kOutput, calls=%fused_computation.48 | convolution fusion | flops 1260847104 | bytes 13389824 | tf_op jit(solution)/shard_map/dot_general | solution.py:485
  353.5 2.8 convert_reduce_fusion.4
  361.3 3.3 multiply_reduce_fusion.4
  369.7 5.2 fusion.315
  377.0 2.4 multiply_reduce_fusion.19
  385.2 5.1 fusion.210
  390.3 3.4 fusion.86.refs_5_
  402.3 5.6 fusion.159
  409.7 6.1 convert_reduce_fusion.3
  424.0 3.5 multiply_reduce_fusion.3
  432.6 5.2 fusion.318
  437.9 5.2 fusion.201
  445.2 2.4 multiply_reduce_fusion.17
  461.6 5.5 fusion.157
  468.0 6.1 convert_reduce_fusion.2
  482.3 3.5 multiply_reduce_fusion.2
  490.8 5.3 fusion.321
  496.1 5.3 fusion.192
  501.4 2.7 multiply_add_fusion.2
  504.2 3.3 multiply_reduce_fusion.15
  521.0 5.5 fusion.155
  528.3 6.1 convert_reduce_fusion.1
  542.7 3.5 multiply_reduce_fusion.1
  551.1 5.2 fusion.324
  556.4 5.5 fusion.183
  564.0 2.4 multiply_reduce_fusion.13
  579.9 5.5 fusion.153
  587.2 6.1 convert_reduce_fusion
  600.0 3.3 multiply_reduce_fusion
  608.6 2.4 multiply_reduce_fusion.11
  689.9 2.6 concatenate.368
  709.6 12.7 %add_convert_fusion.2 = bf16[768,2304]{1,0:T(8,128)(2,1)} fusion(f32[768,2304]{1,0:T(8,128)} %fusion.153, f32[768,2304]{1,0:T(8,128)} %fusion.155, f32[768,2304]{1,0:T(8,128)} %fusion.159, f32[768,2304]{1,0:T(8,128)} %fusion.157, bf16[256,768]{0,1:T(8,128)(2,1)} %bitcast.974, bf16[256,768]{0,1:T(8,128)(2,1)} %bitcast.937, bf16[256,768]{0,1:T(8,128)(2,1)} %bitcast.934, ...), kind=kOutput, calls=%fused_computation.2 | convolution fusion | flops 919732224 | bytes 33433600 | tf_op jit(solution)/shard_map/bpd,bpe->de/dot_general | solution.py:607
  722.4 3.6 add_convert_fusion.8
  726.0 15.8 %add_convert_fusion = bf16[768,3072]{1,0:T(8,128)(2,1)} fusion(f32[768,3072]{1,0:T(8,128)} %fusion.324, f32[768,3072]{1,0:T(8,128)} %fusion.321, f32[768,3072]{1,0:T(8,128)} %fusion.315, f32[768,3072]{1,0:T(8,128)} %fusion.318, bf16[256,3072]{1,0:T(8,128)(2,1)} %copy-done.117, f32[1,256,768]{2,1,0:T(8,128)S(1)} %copy-done.62, f32[768]{0:T(1024)S(1)} %copy-done.150, ...), kind=kOutput, calls=%fused_computation | convolution fusion | flops 1220739072 | bytes 44834816 | tf_op jit(solution)/shard_map/bpd,bpf->df/dot_general | solution.py:553
  741.8 15.4 %add_convert_fusion.1 = bf16[3072,768]{1,0:T(8,128)(2,1)} fusion(f32[3072,768]{1,0:T(8,128)} %fusion.183, f32[3072,768]{1,0:T(8,128)} %fusion.192, f32[3072,768]{1,0:T(8,128)} %fusion.210, f32[3072,768]{1,0:T(8,128)} %fusion.201, bf16[256,3072]{1,0:T(8,128)(2,1)S(1)} %copy-done.116, bf16[1,256,768]{2,1,0:T(8,128)(2,1)S(1)} %copy-done.73, ...), kind=kOutput, calls=%fused_computation.1 | convolution fusion | flops 1220542464 | bytes 44434432 | tf_op jit(solution)/shard_map/bpf,bpd->fd/dot_general | solution.py:546
  757.2 124.9 %reduce.123 = (f32[384,768]{1,0:T(8,128)}, f32[96,3072]{1,0:T(8,128)}, f32[96,768]{1,0:T(8,128)}, f32[96,2304]{1,0:T(8,128)}, f32[16,128]{1,0:T(8,128)}, /*index=5*/f32[2,256,768]{2,1,0:T(8,128)}, f32[2,256,768]{2,1,0:T(8,128)}) custom-call(bf16[8,384,768]{2,1,0:T(8,128)(2,1)} %bitcast.885, bf16[8,96,3072]{2,1,0:T(8,128)(2,1)} %bitcast.884, ...), custom_call_target="tpu_custom_call" | custom-call | tf_op jit(solution)/shard_map/reduce/pallas_call | solution.py:367
  885.4 2.7 copy.215
  (1227 shorter events, 305.4 us)
Async XLA Ops:
  143.1 93.4 %copy-start.151 = (f32[768]{0:T(1024)}, f32[768]{0:T(1024)S(1)}, u32[]{:S(2)}) copy-start(f32[768]{0:T(1024)S(1)} %reshape.3400) | copy-start | bytes 9220
  149.3 49.0 %copy-start.263 = (f32[1,256]{1,0:T(1,128)}, f32[1,256]{1,0:T(1,128)S(1)}, u32[]{:S(2)}) copy-start(f32[1,256]{1,0:T(1,128)S(1)} %get-tuple-element.297) | copy-start | bytes 3076
  149.5 92.8 %copy-start.108 = (f32[12,32]{1,0:T(8,128)}, f32[12,32]{1,0:T(8,128)S(1)}, u32[]{:S(2)}) copy-start(f32[12,32]{1,0:T(8,128)S(1)} %mul.1989) | copy-start | bytes 4612
  150.0 23.5 %copy-start.258 = (f32[1,1,256]{2,1,0:T(1,128)}, f32[1,1,256]{2,1,0:T(1,128)S(1)}, u32[]{:S(2)}) copy-start(f32[1,1,256]{2,1,0:T(1,128)S(1)} %get-tuple-element.305) | copy-start | bytes 3076
  150.0 70.7 %copy-start.296 = (f32[1,1,256]{2,1,0:T(1,128)}, f32[1,1,256]{2,1,0:T(1,128)S(1)}, u32[]{:S(2)}) copy-start(f32[1,1,256]{2,1,0:T(1,128)S(1)} %get-tuple-element.304) | copy-start | bytes 3076
  150.0 78.9 %copy-start.299 = (f32[1,1,256]{2,1,0:T(1,128)}, f32[1,1,256]{2,1,0:T(1,128)S(1)}, u32[]{:S(2)}) copy-start(f32[1,1,256]{2,1,0:T(1,128)S(1)} %get-tuple-element.303) | copy-start | bytes 3076
  156.0 51.6 %copy-start.379 = (f32[768]{0:T(1024)}, f32[768]{0:T(1024)S(1)}, u32[]{:S(2)}) copy-start(f32[768]{0:T(1024)S(1)} %reshape.3402) | copy-start | bytes 9220
  159.7 13.8 %copy-start.60 = (f32[1,256,768]{2,1,0:T(8,128)}, f32[1,256,768]{2,1,0:T(8,128)S(1)}, u32[]{:S(2)}) copy-start(f32[1,256,768]{2,1,0:T(8,128)S(1)} %get-tuple-element.316) | copy-start | bytes 2359300
  159.8 12.4 %copy-start.255 = (f32[256]{0:T(256)}, f32[256]{0:T(256)S(1)}, u32[]{:S(2)}) copy-start(f32[256]{0:T(256)S(1)} %broadcast_multiply_fusion.8) | copy-start | bytes 3076
  160.0 12.2 %copy-start.328 = (f32[256]{0:T(256)}, f32[256]{0:T(256)S(1)}, u32[]{:S(2)}) copy-start(f32[256]{0:T(256)S(1)} %fusion.266) | copy-start | bytes 3076
  160.7 47.9 %copy-start.142 = (f32[768]{0:T(1024)}, f32[768]{0:T(1024)S(1)}, u32[]{:S(2)}) copy-start(f32[768]{0:T(1024)S(1)} %reshape.3404) | copy-start | bytes 9220
  160.8 47.9 %copy-start.322 = (f32[3072]{0:T(1024)}, f32[3072]{0:T(1024)S(1)}, u32[]{:S(2)}) copy-start(f32[3072]{0:T(1024)S(1)} %reshape.3405) | copy-start | bytes 36868
  160.9 59.9 %copy-start.375 = (f32[768]{0:T(1024)}, f32[768]{0:T(1024)S(1)}, u32[]{:S(2)}) copy-start(f32[768]{0:T(1024)S(1)} %reshape.3406) | copy-start | bytes 9220
  178.2 12.6 %collective-permute-start = (bf16[1,256,768]{2,1,0:T(8,128)(2,1)S(1)}, bf16[1,256,768]{2,1,0:T(8,128)(2,1)S(1)}, u32[]{:S(2)}, u32[]{:S(2)}) collective-permute-start(bf16[1,256,768]{2,1,0:T(8,128)(2,1)S(1)} %get-tuple-element.191), channel_id=1, source_target_pairs={{0,2},{1,3},{2,16},{3,17},{4,6},{5,7},{6,20},{7,21},{8,10},{9,11},... | collective-permute-start | bytes 1179656 | tf_op jit(solution)/shard_map/ppermute | solution.py:713
  182.8 21.9 %copy-start.365 = (pred[256]{0:T(512)(128)(4,1)}, pred[256]{0:T(512)(128)(4,1)S(1)}, u32[]{:S(2)}) copy-start(pred[256]{0:T(512)(128)(4,1)S(1)} %broadcast_compare_fusion.3) | copy-start | bytes 772
  182.8 15.4 %copy-start.270 = (f32[1,256]{1,0:T(1,128)}, f32[1,256]{1,0:T(1,128)S(1)}, u32[]{:S(2)}) copy-start(f32[1,256]{1,0:T(1,128)S(1)} %fusion.251) | copy-start | bytes 3076
  191.0 16.7 %copy-start.12 = (bf16[1,256,768]{2,1,0:T(8,128)(2,1)}, bf16[1,256,768]{2,1,0:T(8,128)(2,1)S(1)}, u32[]{:S(2)}) copy-start(bf16[1,256,768]{2,1,0:T(8,128)(2,1)S(1)} %get-tuple-element.128) | copy-start | bytes 1179652
  207.7 13.1 %slice-start.10 = ((s8[4718592]{0:T(1024)(128)(4,1)}), s8[4194304]{0:T(1024)(128)(4,1)S(1)}, s32[]{:S(2)}) async-start(s8[4718592]{0:T(1024)(128)(4,1)} %bitcast.1105), calls=%async_computation.10 | async-start | bytes 8388608
  208.3 12.5 %copy-start.63 = (f32[1,256,768]{2,1,0:T(8,128)}, f32[1,256,768]{2,1,0:T(8,128)S(1)}, u32[]{:S(2)}) copy-start(f32[1,256,768]{2,1,0:T(8,128)S(1)} %get-tuple-element.322) | copy-start | bytes 2359300
  208.3 12.4 %copy-start.244 = (f32[256]{0:T(256)}, f32[256]{0:T(256)S(1)}, u32[]{:S(2)}) copy-start(f32[256]{0:T(256)S(1)} %broadcast_multiply_fusion.6) | copy-start | bytes 3076
  220.8 15.7 %copy-start.388 = (bf16[8,96,2304]{2,1,0:T(8,128)(2,1)S(1)}, bf16[8,96,2304]{2,1,0:T(8,128)(2,1)}, u32[]{:S(2)}) copy-start(bf16[8,96,2304]{2,1,0:T(8,128)(2,1)} %get-tuple-element.33) | copy-start | bytes 10616836
  224.8 11.2 %collective-permute-start.1 = (bf16[1,256,768]{2,1,0:T(8,128)(2,1)S(1)}, bf16[1,256,768]{2,1,0:T(8,128)(2,1)S(1)}, u32[]{:S(2)}, u32[]{:S(2)}) collective-permute-start(bf16[1,256,768]{2,1,0:T(8,128)(2,1)S(1)} %get-tuple-element.189), channel_id=1, source_target_pairs={{0,2},{1,3},{2,16},{3,17},{4,6},{5,7},{6,20},{7,21},{8,10},{9,11},... | collective-permute-start | bytes 1179656 | tf_op jit(solution)/shard_map/ppermute | solution.py:713
  229.5 12.7 %copy-start.272 = (f32[1,256]{1,0:T(1,128)}, f32[1,256]{1,0:T(1,128)S(1)}, u32[]{:S(2)}) copy-start(f32[1,256]{1,0:T(1,128)S(1)} %fusion.252) | copy-start | bytes 3076
  236.1 16.1 %copy-start.14 = (bf16[1,256,768]{2,1,0:T(8,128)(2,1)}, bf16[1,256,768]{2,1,0:T(8,128)(2,1)S(1)}, u32[]{:S(2)}) copy-start(bf16[1,256,768]{2,1,0:T(8,128)(2,1)S(1)} %collective-permute-done.1) | copy-start | bytes 1179652
  252.2 13.1 %copy-start.202 = (bf16[12,64,256]{2,1,0:T(8,128)(2,1)}, bf16[12,64,256]{2,1,0:T(8,128)(2,1)S(1)}, u32[]{:S(2)}) copy-start(bf16[12,64,256]{2,1,0:T(8,128)(2,1)S(1)} %convolution_convert_fusion.12) | copy-start | bytes 1179652
  252.2 13.1 %slice-start.12 = ((s8[4718592]{0:T(1024)(128)(4,1)}), s8[4194304]{0:T(1024)(128)(4,1)S(1)}, s32[]{:S(2)}) async-start(s8[4718592]{0:T(1024)(128)(4,1)} %bitcast.1108), calls=%async_computation.12 | async-start | bytes 8388608
  252.9 12.4 %copy-start.65 = (f32[1,256,768]{2,1,0:T(8,128)}, f32[1,256,768]{2,1,0:T(8,128)S(1)}, u32[]{:S(2)}) copy-start(f32[1,256,768]{2,1,0:T(8,128)S(1)} %get-tuple-element.328) | copy-start | bytes 2359300
  252.9 12.4 %copy-start.247 = (f32[256]{0:T(256)}, f32[256]{0:T(256)S(1)}, u32[]{:S(2)}) copy-start(f32[256]{0:T(256)S(1)} %broadcast_multiply_fusion.4) | copy-start | bytes 3076
  265.4 15.9 %copy-start.152 = (f32[768]{0:T(1024)S(1)}, f32[768]{0:T(1024)}, u32[]{:S(2)}) copy-start(f32[768]{0:T(1024)} %copy-done.151) | copy-start | bytes 9220
  265.4 15.9 %copy-start.389 = (bf16[8,96,2304]{2,1,0:T(8,128)(2,1)S(1)}, bf16[8,96,2304]{2,1,0:T(8,128)(2,1)}, u32[]{:S(2)}) copy-start(bf16[8,96,2304]{2,1,0:T(8,128)(2,1)} %get-tuple-element.33) | copy-start | bytes 10616836
  269.4 10.4 %collective-permute-start.2 = (bf16[1,256,768]{2,1,0:T(8,128)(2,1)S(1)}, bf16[1,256,768]{2,1,0:T(8,128)(2,1)S(1)}, u32[]{:S(2)}, u32[]{:S(2)}) collective-permute-start(bf16[1,256,768]{2,1,0:T(8,128)(2,1)S(1)} %get-tuple-element.187), channel_id=1, source_target_pairs={{0,2},{1,3},{2,16},{3,17},{4,6},{5,7},{6,20},{7,21},{8,10},{9,11},... | collective-permute-start | bytes 1179656 | tf_op jit(solution)/shard_map/ppermute | solution.py:713
  274.0 12.9 %copy-start.274 = (f32[1,256]{1,0:T(1,128)}, f32[1,256]{1,0:T(1,128)S(1)}, u32[]{:S(2)}) copy-start(f32[1,256]{1,0:T(1,128)S(1)} %fusion.253) | copy-start | bytes 3076
  293.6 15.4 %slice-start.14 = ((s8[4718592]{0:T(1024)(128)(4,1)}), s8[4194304]{0:T(1024)(128)(4,1)S(1)}, s32[]{:S(2)}) async-start(s8[4718592]{0:T(1024)(128)(4,1)} %bitcast.1111), calls=%async_computation.14 | async-start | bytes 8388608
  296.5 12.4 %copy-start.204 = (bf16[12,64,256]{2,1,0:T(8,128)(2,1)}, bf16[12,64,256]{2,1,0:T(8,128)(2,1)S(1)}, u32[]{:S(2)}) copy-start(bf16[12,64,256]{2,1,0:T(8,128)(2,1)S(1)} %convolution_convert_fusion.11) | copy-start | bytes 1179652
  309.0 15.8 %copy-start.153 = (f32[768]{0:T(1024)S(1)}, f32[768]{0:T(1024)}, u32[]{:S(2)}) copy-start(f32[768]{0:T(1024)} %copy-done.151) | copy-start | bytes 9220
  309.0 15.8 %copy-start.390 = (bf16[8,96,2304]{2,1,0:T(8,128)(2,1)S(1)}, bf16[8,96,2304]{2,1,0:T(8,128)(2,1)}, u32[]{:S(2)}) copy-start(bf16[8,96,2304]{2,1,0:T(8,128)(2,1)} %get-tuple-element.33) | copy-start | bytes 10616836
  313.0 10.3 %collective-permute-start.3 = (bf16[1,256,768]{2,1,0:T(8,128)(2,1)S(1)}, bf16[1,256,768]{2,1,0:T(8,128)(2,1)S(1)}, u32[]{:S(2)}, u32[]{:S(2)}) collective-permute-start(bf16[1,256,768]{2,1,0:T(8,128)(2,1)S(1)} %get-tuple-element.185), channel_id=1, source_target_pairs={{0,2},{1,3},{2,16},{3,17},{4,6},{5,7},{6,20},{7,21},{8,10},{9,11},... | collective-permute-start | bytes 1179656 | tf_op jit(solution)/shard_map/ppermute | solution.py:713
  338.5 14.9 %slice-start.16 = ((s8[4718592]{0:T(1024)(128)(4,1)}), s8[4194304]{0:T(1024)(128)(4,1)S(1)}, s32[]{:S(2)}) async-start(s8[4718592]{0:T(1024)(128)(4,1)} %bitcast.1114), calls=%async_computation.16 | async-start | bytes 8388608
  338.5 17.8 %slice-start = ((s8[4718592]{0:T(1024)(128)(4,1)}), s8[4194304]{0:T(1024)(128)(4,1)S(1)}, s32[]{:S(2)}) async-start(s8[4718592]{0:T(1024)(128)(4,1)} %bitcast.1085), calls=%async_computation | async-start | bytes 8388608
  342.1 16.4 %copy-start.70 = (f32[1,256,768]{2,1,0:T(8,128)}, f32[1,256,768]{2,1,0:T(8,128)S(1)}, u32[]{:S(2)}) copy-start(f32[1,256,768]{2,1,0:T(8,128)S(1)} %get-tuple-element.340) | copy-start | bytes 2359300
  342.1 16.4 %copy-start.253 = (f32[256]{0:T(256)}, f32[256]{0:T(256)S(1)}, u32[]{:S(2)}) copy-start(f32[256]{0:T(256)S(1)} %broadcast_multiply_fusion) | copy-start | bytes 3076
  342.4 16.1 %copy-start.317 = (f32[256]{0:T(256)}, f32[256]{0:T(256)S(1)}, u32[]{:S(2)}) copy-start(f32[256]{0:T(256)S(1)} %fusion.274) | copy-start | bytes 3076
  342.4 13.9 %slice-start.1 = ((s8[4718592]{0:T(1024)(128)(4,1)}), s8[524288]{0:T(1024)(128)(4,1)S(1)}, s32[]{:S(2)}) async-start(s8[4718592]{0:T(1024)(128)(4,1)} %bitcast.1085), calls=%async_computation.1 | async-start | bytes 1048576
  383.5 24.4 %collective-permute-start.4 = (bf16[1,256,768]{2,1,0:T(8,128)(2,1)}, bf16[1,256,768]{2,1,0:T(8,128)(2,1)}, u32[]{:S(2)}, u32[]{:S(2)}) collective-permute-start(bf16[1,256,768]{2,1,0:T(8,128)(2,1)} %get-tuple-element.82), channel_id=1, source_target_pairs={{2,0},{3,1},{6,4},{7,5},{10,8},{11,9},{14,12},{15,13},{16,2},{17,3... | collective-permute-start | bytes 1179656 | tf_op jit(solution)/shard_map/ppermute | solution.py:733
  402.3 13.5 %slice-start.2 = ((s8[4718592]{0:T(1024)(128)(4,1)}), s8[4194304]{0:T(1024)(128)(4,1)S(1)}, s32[]{:S(2)}) async-start(s8[4718592]{0:T(1024)(128)(4,1)} %bitcast.1088), calls=%async_computation.2 | async-start | bytes 8388608
  430.7 17.0 %copy-start.138 = (bf16[12,64,256]{2,1,0:T(8,128)(2,1)}, bf16[12,64,256]{2,1,0:T(8,128)(2,1)S(1)}, u32[]{:S(2)}) copy-start(bf16[12,64,256]{2,1,0:T(8,128)(2,1)S(1)} %convolution_convert_fusion.6) | copy-start | bytes 1179652
  451.4 15.7 %collective-permute-start.5 = (bf16[1,256,768]{2,1,0:T(8,128)(2,1)}, bf16[1,256,768]{2,1,0:T(8,128)(2,1)S(1)}, u32[]{:S(2)}, u32[]{:S(2)}) collective-permute-start(bf16[1,256,768]{2,1,0:T(8,128)(2,1)} %get-tuple-element.80), channel_id=1, source_target_pairs={{2,0},{3,1},{6,4},{7,5},{10,8},{11,9},{14,12},{15,13},{16,2},{17,3... | collective-permute-start | bytes 1179656 | tf_op jit(solution)/shard_map/ppermute | solution.py:733
  461.6 12.5 %slice-start.4 = ((s8[4718592]{0:T(1024)(128)(4,1)}), s8[4194304]{0:T(1024)(128)(4,1)S(1)}, s32[]{:S(2)}) async-start(s8[4718592]{0:T(1024)(128)(4,1)} %bitcast.1091), calls=%async_computation.4 | async-start | bytes 8388608
  488.8 18.8 %copy-start.139 = (bf16[12,64,256]{2,1,0:T(8,128)(2,1)}, bf16[12,64,256]{2,1,0:T(8,128)(2,1)S(1)}, u32[]{:S(2)}) copy-start(bf16[12,64,256]{2,1,0:T(8,128)(2,1)S(1)} %convolution_convert_fusion.4) | copy-start | bytes 1179652
  511.3 15.2 %collective-permute-start.6 = (bf16[1,256,768]{2,1,0:T(8,128)(2,1)}, bf16[1,256,768]{2,1,0:T(8,128)(2,1)}, u32[]{:S(2)}, u32[]{:S(2)}) collective-permute-start(bf16[1,256,768]{2,1,0:T(8,128)(2,1)} %get-tuple-element.78), channel_id=1, source_target_pairs={{2,0},{3,1},{6,4},{7,5},{10,8},{11,9},{14,12},{15,13},{16,2},{17,3... | collective-permute-start | bytes 1179656 | tf_op jit(solution)/shard_map/ppermute | solution.py:733
  521.0 13.4 %slice-start.6 = ((s8[4718592]{0:T(1024)(128)(4,1)}), s8[4194304]{0:T(1024)(128)(4,1)S(1)}, s32[]{:S(2)}) async-start(s8[4718592]{0:T(1024)(128)(4,1)} %bitcast.1094), calls=%async_computation.6 | async-start | bytes 8388608
  549.2 17.3 %copy-start.140 = (bf16[12,64,256]{2,1,0:T(8,128)(2,1)}, bf16[12,64,256]{2,1,0:T(8,128)(2,1)S(1)}, u32[]{:S(2)}) copy-start(bf16[12,64,256]{2,1,0:T(8,128)(2,1)S(1)} %convolution_convert_fusion.2) | copy-start | bytes 1179652
  570.2 15.2 %collective-permute-start.7 = (bf16[1,256,768]{2,1,0:T(8,128)(2,1)}, bf16[1,256,768]{2,1,0:T(8,128)(2,1)}, u32[]{:S(2)}, u32[]{:S(2)}) collective-permute-start(bf16[1,256,768]{2,1,0:T(8,128)(2,1)} %get-tuple-element.76), channel_id=1, source_target_pairs={{2,0},{3,1},{6,4},{7,5},{10,8},{11,9},{14,12},{15,13},{16,2},{17,3... | collective-permute-start | bytes 1179656 | tf_op jit(solution)/shard_map/ppermute | solution.py:733
  579.9 13.4 %slice-start.8 = ((s8[4718592]{0:T(1024)(128)(4,1)}), s8[4194304]{0:T(1024)(128)(4,1)S(1)}, s32[]{:S(2)}) async-start(s8[4718592]{0:T(1024)(128)(4,1)} %bitcast.1097), calls=%async_computation.8 | async-start | bytes 8388608
  612.6 81.1 %copy-start.73 = (bf16[1,256,768]{2,1,0:T(8,128)(2,1)S(1)}, bf16[1,256,768]{2,1,0:T(8,128)(2,1)}, u32[]{:S(2)}) copy-start(bf16[1,256,768]{2,1,0:T(8,128)(2,1)} %copy-done.72) | copy-start | bytes 1179652
  615.0 94.6 %copy-start.154 = (f32[768]{0:T(1024)S(1)}, f32[768]{0:T(1024)}, u32[]{:S(2)}) copy-start(f32[768]{0:T(1024)} %copy-done.151) | copy-start | bytes 9220
  695.5 26.8 %copy-start.11 = (f32[2,256,768]{2,1,0:T(8,128)}, f32[2,256,768]{2,1,0:T(8,128)S(1)}, u32[]{:S(2)}) copy-start(f32[2,256,768]{2,1,0:T(8,128)S(1)} %select_dynamic-update-slice_fusion.refs_6_) | copy-start | bytes 4718596
  709.6 12.7 %copy-start.24 = (f32[768,768]{1,0:T(8,128)S(1)}, f32[768,768]{1,0:T(8,128)}, u32[]{:S(2)}) copy-start(f32[768,768]{1,0:T(8,128)} %fusion.205) | copy-start | bytes 7077892
  709.6 12.7 %copy-start.25 = (f32[768,768]{1,0:T(8,128)S(1)}, f32[768,768]{1,0:T(8,128)}, u32[]{:S(2)}) copy-start(f32[768,768]{1,0:T(8,128)} %fusion.196) | copy-start | bytes 7077892
  709.6 12.7 %copy-start.26 = (f32[768,768]{1,0:T(8,128)S(1)}, f32[768,768]{1,0:T(8,128)}, u32[]{:S(2)}) copy-start(f32[768,768]{1,0:T(8,128)} %fusion.187) | copy-start | bytes 7077892
  709.6 12.7 %copy-start.79 = (bf16[1,256,768]{2,1,0:T(8,128)(2,1)S(1)}, bf16[1,256,768]{2,1,0:T(8,128)(2,1)}, u32[]{:S(2)}) copy-start(bf16[1,256,768]{2,1,0:T(8,128)(2,1)} %copy-done.78) | copy-start | bytes 1179652
  709.6 12.7 %copy-start.199 = (bf16[12,64,256]{2,1,0:T(8,128)(2,1)S(1)}, bf16[12,64,256]{2,1,0:T(8,128)(2,1)}, u32[]{:S(2)}) copy-start(bf16[12,64,256]{2,1,0:T(8,128)(2,1)} %copy-done.198) | copy-start | bytes 1179652
  726.0 15.8 %copy-start.116 = (bf16[256,3072]{1,0:T(8,128)(2,1)S(1)}, bf16[256,3072]{1,0:T(8,128)(2,1)}, u32[]{:S(2)}) copy-start(bf16[256,3072]{1,0:T(8,128)(2,1)} %copy-done.115) | copy-start | bytes 4718596
  726.0 15.8 %copy-start.260 = (f32[1,1,256]{2,1,0:T(1,128)S(1)}, f32[1,1,256]{2,1,0:T(1,128)}, u32[]{:S(2)}) copy-start(f32[1,1,256]{2,1,0:T(1,128)} %copy-done.258) | copy-start | bytes 3076
  (364 other events, 1372.3 us)

commit v2 on v0

v2 whole, which is shorter than its diff:
```python
import functools
import math

import jax
import jax.numpy as jnp
from jax import lax
from jax.experimental import pallas as pl
from jax.experimental.pallas import tpu as pltpu
from jax.sharding import PartitionSpec as P

D = 768
H = 12
HD = 64
GRID = 16
EPSILON = 1e-06
MASKED = -1e30
GROUPS = 8
LANES = 128
TILE = 256
CHUNK = 64
MESH = pl.DeviceIdType.MESH
F32 = jnp.float32
LOW = jnp.bfloat16


class Place:
    def __init__(self, replicas):
        section = lax.axis_index("section")
        dp = lax.axis_index("dp")
        self.replicas = replicas
        self.x, self.core = lax.div(section, 2), lax.rem(section, 2)
        group, self.m = lax.div(dp, replicas), lax.rem(dp, replicas)
        self.z, self.y = lax.div(group, 2), lax.rem(group, 2)
        self.half, self.odd = lax.div(self.z, 2), lax.rem(self.z, 2)
        self.role = 2 * self.x + self.odd
        self.mine = 2 * self.z + self.y
        self.home = self.core == self.odd
        self.away = self.core != self.odd

    def device(self, x, core, z, y):
        return (2 * x + core, (2 * z + y) * self.replicas + self.m)

    def sibling(self):
        return self.device(self.x, 1 - self.core, self.z, self.y)

    def across(self):
        return self.device(self.x, self.core, self.z, 1 - self.y)

    def along(self, k):
        return self.device(self.x, self.odd, self.core + 2 * k, self.y)

    def twin(self):
        return self.along(self.half)

    def is_self(self, k):
        return jnp.logical_and(self.home, self.half == k)

    def section(self, role):
        return self.device(
            lax.div(role, 2), self.core, 2 * self.half + lax.rem(role, 2), self.y
        )


def remote(source, target, send, arrive, to):
    return pltpu.make_async_remote_copy(
        src_ref=source,
        dst_ref=target,
        send_sem=send,
        recv_sem=arrive,
        device_id=to,
        device_id_type=MESH,
    )


def enter(at, sections):
    barrier = pltpu.get_barrier_semaphore()

    def greet(to):
        pl.semaphore_signal(barrier, inc=1, device_id=to, device_id_type=MESH)

    greet(at.sibling())
    greet(at.across())
    for k in range(2):

        @pl.when(jnp.logical_not(at.is_self(k)))
        def _():
            greet(at.along(k))

    @pl.when(at.role > 0)
    def _():
        greet(at.section(at.role - 1))

    @pl.when(at.role < sections - 1)
    def _():
        greet(at.section(at.role + 1))

    ends = jnp.where(jnp.logical_or(at.role == 0, at.role == sections - 1), 1, 0)
    pl.semaphore_wait(barrier, 6 - jnp.where(at.home, 1, 0) - ends)


def span(start, size):
    return pl.ds(pl.multiple_of(start, size), size)


def dot(a, b):
    return jnp.dot(a, b, preferred_element_type=F32)


def dot_nt(a, b):
    return lax.dot_general(a, b, (((1,), (1,)), ((), ())), preferred_element_type=F32)


def dot_tn(a, b):
    return lax.dot_general(a, b, (((0,), (0,)), ((), ())), preferred_element_type=F32)


def loop(count, body):
    def step(i, carry):
        body(i)
        return carry

    lax.fori_loop(0, count, step, 0)


SMALL_ROWS = 16


def quotient(values, divisor):
    return jnp.floor((values + 0.5) * (1.0 / divisor))


def selectors(size, first_row, index):
    group = quotient(index, size)
    inside = index - group * size
    row_in = quotient(inside, LANES)
    lane = inside - row_in * LANES
    row = group * SMALL_ROWS + as_float(first_row) + row_in
    ids = lax.broadcasted_iota(jnp.int32, (GROUPS * SMALL_ROWS, index.shape[1]), 0).astype(F32)
    return (ids == row).astype(F32), (ids == lane).astype(F32)


def positions(count):
    return lax.broadcasted_iota(jnp.int32, (1, count), 1).astype(F32)


def as_float(value):
    return lax.convert_element_type(value, F32)


def spread_positions():
    at = positions(D)
    head = quotient(at, HD)
    inside = at - head * HD
    return head * (HD // 2) + inside - quotient(inside, HD // 2) * (HD // 2)


def expand(block, size, first_row, index):
    rows, lanes = selectors(size, first_row, index)
    values = dot(block, lanes.astype(LOW))
    return jnp.sum(values * rows, axis=0, keepdims=True)


def fold(vector, size, first_row, index):
    rows, lanes = selectors(size, first_row, index)
    return lax.dot_general(
        rows * vector,
        lanes,
        (((1,), (1,)), ((), ())),
        precision=lax.Precision.HIGHEST,
        preferred_element_type=F32,
    )


def normalise(values):
    mean = jnp.mean(values, axis=-1, keepdims=True)
    centred = values - mean
    variance = jnp.mean(centred * centred, axis=-1, keepdims=True)
    scale = lax.rsqrt(variance + EPSILON)
    return centred * scale, scale


def first_half(shape):
    return jnp.bitwise_and(lax.broadcasted_iota(jnp.int32, shape, 1), HD - 1) < HD // 2


def partner(values):
    left = pltpu.roll(values, values.shape[1] - HD // 2, 1)
    right = pltpu.roll(values, HD // 2, 1)
    return jnp.where(first_half(values.shape), left, right)


def unfold_turn(table):
    first, other = first_half(table.shape), partner(table)
    return jnp.where(first, table, other), jnp.where(first, -other, table)


def gelu_pair(u):
    phi = 0.5 * (1.0 + lax.erf(u * math.sqrt(0.5)))
    density = jnp.exp(-0.5 * u * u) * (1.0 / math.sqrt(2.0 * math.pi))
    return u * phi, phi + u * density


GAIN_ONE, SHIFT_ONE, PROJ_SHIFT, GAIN_TWO, SHIFT_TWO, DOWN_SHIFT, FREQ_ROW, FREQ_COL = range(8)


def block_kernel(replicas, sections, images_here, patches, *refs):
    ins, refs = refs[:9], refs[9:]
    outs, refs = refs[:7], refs[7:]
    parts = ins[:5]
    images, cotangent, facts_col, facts_row = ins[5:]
    result_out, grad_out_ref = outs[:2]
    sums = outs[2:]
    (
        qkv_w, proj_w, up_w, down_w, small_w,
        first_0, first_1, first_2, first_3, first_4,
        second_0, second_1, second_2, second_3, second_4,
        third_0, third_1, third_2, third_3, third_4,
        xin, gin, fcol, frow, qkv, probs, att, mid, n2, act, slope, g1, wide,
        shipped, stage, turns, vec, qkv_b, up_b, vec_g, qkv_bg, up_bg, small_f,
        gather_send, gather_arrive, reduce_send, reduce_arrive,
        swap_send, swap_arrive, pipe_send, pipe_arrive, ship_send, ship_arrive, tile_sem,
    ) = refs
    wholes = (small_w, qkv_w, proj_w, up_w, down_w)
    shares = (parts[4], parts[0], parts[1], parts[2], parts[3])
    firsts = (first_4, first_0, first_1, first_2, first_3)
    seconds = (second_4, second_0, second_1, second_2, second_3)
    thirds = (third_4, third_0, third_1, third_2, third_3)
    totals = (sums[4], sums[0], sums[1], sums[2], sums[3])
    partials = (small_f, qkv_w, proj_w, up_w, down_w)
    at = Place(replicas)
    last = sections - 1

    enter(at, sections)

    def swap_copy(n, source, target):
        return remote(source, target, swap_send.at[n], swap_arrive.at[n], at.twin())

    def swap_local(n, source, target):
        return pltpu.make_async_copy(source, target, swap_arrive.at[n])

    every = at.core >= 0
    moves = (
        (0, facts_col, fcol, every, every),
        (1, facts_row, frow, every, every),
        (
            2, images, xin,
            jnp.logical_and(at.x == 0, at.core == 0),
            at.role == 0,
        ),
        (
            3, cotangent, gin,
            jnp.logical_and(at.x == last // 2, at.core == last % 2),
            at.role == last,
        ),
    )

    def swap_start(n):
        number, source, target, sends, takes = moves[n]

        @pl.when(jnp.logical_and(sends, at.home))
        def _():
            swap_local(number, source, target).start()

        @pl.when(jnp.logical_and(sends, at.away))
        def _():
            swap_copy(number, source, target).start()

    def swap_wait(n):
        number, source, target, sends, takes = moves[n]

        @pl.when(jnp.logical_and(takes, at.home))
        def _():
            swap_local(number, source, target).wait()

        @pl.when(jnp.logical_and(takes, at.away))
        def _():
            swap_copy(number, source, target).wait_recv()

    def swap_sent(n):
        number, source, target, sends, takes = moves[n]

        @pl.when(jnp.logical_and(sends, at.away))
        def _():
            swap_copy(number, source, target).wait_send()

    def block_of(ref, group):
        size = ref.shape[0] // GROUPS
        return ref.at[span(group * size, size), :]

    def along(n, k):
        return remote(
            shares[n], block_of(wholes[n], at.mine),
            gather_send.at[n, k], gather_arrive.at[n, at.mine], at.along(k),
        )

    def own(n):
        return pltpu.make_async_copy(
            shares[n], block_of(wholes[n], at.mine), gather_arrive.at[n, at.mine]
        )

    def relay(n, slot, group, to):
        block = block_of(wholes[n], group)
        return remote(block, block, gather_send.at[n, slot], gather_arrive.at[n, group], to)

    def gather_start(n):
        for k in range(2):

            @pl.when(at.is_self(k))
            def _():
                own(n).start()

            @pl.when(jnp.logical_not(at.is_self(k)))
            def _():
                along(n, k).start()

    def gather_relay(n):
        for k in range(2):
            group = 2 * (at.core + 2 * k) + at.y

            @pl.when(at.is_self(k))
            def _():
                own(n).wait()

            @pl.when(jnp.logical_not(at.is_self(k)))
            def _():
                relay(n, 2 + k, group, at.sibling()).wait_recv()

            relay(n, 4 + k, group, at.across()).start()
            relay(n, 2 + k, group, at.sibling()).start()
        for k in range(2):
            group = 2 * (at.core + 2 * k) + 1 - at.y
            relay(n, 6 + k, group, at.sibling()).wait_recv()
            relay(n, 6 + k, group, at.sibling()).start()

    def gather_wait(n):
        for k in range(2):
            for row in range(2):
                group = 2 * (1 - at.core + 2 * k) + row
                relay(n, 2 + k, group, at.sibling()).wait_recv()

    def gather_sent(n):
        for k in range(2):
            group = 2 * (at.core + 2 * k) + at.y
            other = 2 * (at.core + 2 * k) + 1 - at.y

            @pl.when(jnp.logical_not(at.is_self(k)))
            def _():
                along(n, k).wait_send()

            relay(n, 2 + k, group, at.sibling()).wait_send()
            relay(n, 4 + k, group, at.across()).wait_send()
            relay(n, 6 + k, other, at.sibling()).wait_send()

    for n in range(2):
        swap_start(n)
    gather_start(0)
    swap_start(2)
    for n in range(1, 5):
        gather_start(n)
    gather_relay(0)
    gather_wait(0)
    for n in range(2):
        swap_wait(n)

    block = small_w[...]
    q = D // GROUPS
    plain = positions(D)
    apart = spread_positions()

    def take_vector(row):
        vec[row] = expand(block, q, row, plain)

    def take_frequency(t):
        vec[FREQ_ROW + t] = expand(block, q, FREQ_ROW, apart + as_float(t) * (D // 2))

    def take_qkv(t):
        qkv_b[:, span(t * D, D)] = expand(block, 3 * q, 7, plain + as_float(t) * D)

    def take_up(t):
        up_b[:, span(t * D, D)] = expand(block, 4 * q, 10, plain + as_float(t) * D)

    loop(FREQ_ROW, take_vector)
    loop(2, take_frequency)
    loop(3, take_qkv)
    loop(4, take_up)
    vec_g[...] = jnp.zeros_like(vec_g)
    qkv_bg[...] = jnp.zeros_like(qkv_bg)
    up_bg[...] = jnp.zeros_like(up_bg)

    def vector(row):
        return vec[row]

    def vector_at(row, cols):
        return vec[row, :, cols]

    def tables(b):
        rows = span(b * patches, patches)
        facts = fcol[rows, :].astype(F32)
        row_at, col_at = facts[:, 1:2], facts[:, 2:3]
        first = first_half((patches, TILE))

        def piece(t):
            cols = span(t * TILE, TILE)
            angle = row_at * vector_at(FREQ_ROW, cols) + col_at * vector_at(FREQ_COL, cols)
            turns[rows, cols] = jnp.where(first, jnp.cos(angle), jnp.sin(angle))

        loop(D // TILE, piece)

    loop(images_here, tables)

    for n in range(1, 5):
        gather_relay(n)
    swap_start(3)
    for n in range(1, 5):
        gather_wait(n)
    swap_wait(2)

    def ship_start(n, b, source, target):
        rows = span(b * patches, patches)

        @pl.when(at.home)
        def _():
            ship_here(n, b, source, target).start()

        @pl.when(at.away)
        def _():
            ship_away(n, b, source, target).start()

    def ship_here(n, b, source, target):
        rows = span(b * patches, patches)
        return pltpu.make_async_copy(
            source.at[rows, :], target.at[rows, :], ship_arrive.at[n, b]
        )

    def ship_away(n, b, source, target):
        rows = span(b * patches, patches)
        return remote(
            source.at[rows, :], target.at[rows, :],
            ship_send.at[n, b], ship_arrive.at[n, b], at.twin(),
        )

    def ship_wait(n, b, source, target):
        @pl.when(at.home)
        def _():
            ship_here(n, b, source, target).wait()

        @pl.when(at.away)
        def _():
            ship_away(n, b, source, target).wait_recv()
            ship_away(n, b, source, target).wait_send()

    def pipe(n, b, target, role):
        rows = span(b * patches, patches)
        return remote(
            shipped.at[rows, :], target.at[rows, :],
            pipe_send.at[n, b], pipe_arrive.at[n, b], at.section(role),
        )

    def chunks(b, body):
        loop(
            patches // CHUNK,
            lambda i: body(span(b * patches + i * CHUNK, CHUNK), span(i * CHUNK, CHUNK)),
        )

    def forward(b):
        rows = span(b * patches, patches)

        @pl.when(at.role > 0)
        def _():
            pipe(0, b, xin, at.role - 1).wait_recv()

        keep_col = fcol[rows, :].astype(F32)[:, 0:1]
        keep_row = frow[span(b * 8, 8), :][0:1, :]

        def norm_one(here, inside):
            hat, _ = normalise(xin[here, :].astype(F32))
            shipped[here, :] = (hat * vector(GAIN_ONE) + vector(SHIFT_ONE)).astype(LOW)

        chunks(b, norm_one)

        def turn(t):
            cols = span(t * TILE, TILE)
            table = span(lax.rem(t, D // TILE) * TILE, TILE)
            raw = dot(shipped[rows, :], qkv_w[:, cols]) + qkv_b[:, cols]
            cosine, sine = unfold_turn(turns[rows, table])
            turned = raw * cosine + partner(raw) * sine
            qkv[rows, cols] = turned.astype(LOW)

        loop(2 * D // TILE, turn)

        def plain_values(t):
            cols = span(t * TILE + 2 * D, TILE)
            qkv[rows, cols] = (dot(shipped[rows, :], qkv_w[:, cols]) + qkv_b[:, cols]).astype(LOW)

        loop(D // TILE, plain_values)

        def heads(pair):
            cols = span(pair * 2 * HD, 2 * HD)
            query = qkv[rows, cols]
            key = qkv[rows, span(D + pair * 2 * HD, 2 * HD)]
            value = qkv[rows, span(2 * D + pair * 2 * HD, 2 * HD)]
            found = []
            for e in range(2):
                inside = slice(e * HD, (e + 1) * HD)
                scores = dot_nt(query[:, inside], key[:, inside]) * HD ** (-0.5)
                scores = jnp.where(keep_row > 0, scores, MASKED)
                powers = jnp.exp(scores - jnp.max(scores, axis=-1, keepdims=True))
                share = 1.0 / jnp.sum(powers, axis=-1, keepdims=True)
                soft = (powers * share).astype(LOW)
                probs[b * H + 2 * pair + e] = soft
                found.append(dot(soft, value[:, inside]))
            att[rows, cols] = jnp.concatenate(found, axis=-1).astype(LOW)

        loop(H // 2, heads)

        def project(t):
            cols = span(t * TILE, TILE)
            branch = dot(att[rows, :], proj_w[:, cols]) + vector_at(PROJ_SHIFT, cols)
            mid[rows, cols] = xin[rows, cols].astype(F32) + keep_col * branch

        loop(D // TILE, project)

        def norm_two(here, inside):
            hat, _ = normalise(mid[here, :])
            n2[here, :] = (hat * vector(GAIN_TWO) + vector(SHIFT_TWO)).astype(LOW)

        chunks(b, norm_two)

        def raise_tile(t):
            cols = span(t * TILE, TILE)
            hidden = dot(n2[rows, :], up_w[:, cols]) + up_b[:, cols]
            value, gradient = gelu_pair(hidden)
            act[rows, cols] = value.astype(LOW)
            slope[rows, cols] = gradient.astype(LOW)

        loop(up_w.shape[1] // TILE, raise_tile)

        def lower_tile(t):
            cols = span(t * TILE, TILE)
            branch = dot(act[rows, :], down_w[:, cols]) + vector_at(DOWN_SHIFT, cols)
            result = mid[rows, cols] + keep_col * branch
            stage[rows, cols] = result
            shipped[rows, cols] = result.astype(LOW)

        loop(D // TILE, lower_tile)

        @pl.when(at.role < last)
        def _():
            pipe(0, b, xin, at.role + 1).start()

        ship_start(0, b, stage, result_out)

    loop(images_here, forward)

    for b in range(images_here):
        ship_wait(0, b, stage, result_out)

        @pl.when(at.role < last)
        def _():
            pipe(0, b, xin, at.role + 1).wait_send()

    swap_wait(3)
    for n in range(4):
        swap_sent(n)
    for n in range(5):
        gather_sent(n)

    def norm_back(values, gain_row, grad):
        hat, scale = normalise(values)
        vec_g[gain_row] += jnp.sum(grad * hat, axis=0, keepdims=True)
        vec_g[gain_row + 1] += jnp.sum(grad, axis=0, keepdims=True)
        inner = grad * vector(gain_row)
        along_hat = jnp.mean(inner * hat, axis=-1, keepdims=True)
        level = jnp.mean(inner, axis=-1, keepdims=True)
        return scale * (inner - level - hat * along_hat), hat

    def add_row(ref, cols, values):
        ref[:, cols] += jnp.sum(values.astype(F32), axis=0, keepdims=True)

    def backward(b):
        rows = span(b * patches, patches)

        @pl.when(at.role < last)
        def _():
            pipe(1, b, gin, at.role + 1).wait_recv()

        facts = fcol[rows, :].astype(F32)
        row_at, col_at = facts[:, 1:2], facts[:, 2:3]

        def mask_coming(here, inside):
            coming = gin[here, :].astype(F32)
            stage[here, :] = coming
            grad_two = (coming * fcol[here, :].astype(F32)[:, 0:1]).astype(LOW)
            gin[here, :] = grad_two
            vec_g[DOWN_SHIFT] += jnp.sum(grad_two.astype(F32), axis=0, keepdims=True)

        chunks(b, mask_coming)

        def hidden_tile(t):
            cols = span(t * TILE, TILE)
            grad = dot_nt(gin[rows, :], down_w[cols, :])
            low = (grad * slope[rows, cols].astype(F32)).astype(LOW)
            slope[rows, cols] = low
            add_row(up_bg, cols, low)

        loop(up_w.shape[1] // TILE, hidden_tile)

        def normed_two_tile(t):
            cols = span(t * TILE, TILE)
            wide[:, cols] = dot_nt(slope[rows, :], up_w[cols, :])

        loop(D // TILE, normed_two_tile)

        def middle_back(here, inside):
            part, _ = norm_back(mid[here, :], GAIN_TWO, wide[inside, :])
            grad_mid = stage[here, :] + part
            mid[here, :] = grad_mid
            grad_one = (grad_mid * fcol[here, :].astype(F32)[:, 0:1]).astype(LOW)
            g1[here, :] = grad_one
            vec_g[PROJ_SHIFT] += jnp.sum(grad_one.astype(F32), axis=0, keepdims=True)

        chunks(b, middle_back)

        def attended_tile(t):
            cols = span(t * TILE, TILE)
            shipped[rows, cols] = dot_nt(g1[rows, :], proj_w[cols, :]).astype(LOW)

        loop(D // TILE, attended_tile)

        def heads(pair):
            cols = span(pair * 2 * HD, 2 * HD)
            key_cols = span(D + pair * 2 * HD, 2 * HD)
            value_cols = span(2 * D + pair * 2 * HD, 2 * HD)
            query, key, value = qkv[rows, cols], qkv[rows, key_cols], qkv[rows, value_cols]
            grad = shipped[rows, cols]
            to_q, to_k, to_v = [], [], []
            for e in range(2):
                inside = slice(e * HD, (e + 1) * HD)
                soft_low = probs[b * H + 2 * pair + e]
                soft = soft_low.astype(F32)
                grad_soft = dot_nt(grad[:, inside], value[:, inside])
                centre = jnp.sum(soft * grad_soft, axis=-1, keepdims=True)
                grad_scores = (soft * (grad_soft - centre)).astype(LOW)
                to_v.append(dot_tn(soft_low, grad[:, inside]))
                to_q.append(dot(grad_scores, key[:, inside]))
                to_k.append(dot_tn(grad_scores, query[:, inside]))
            turned_q = jnp.concatenate(to_q, axis=-1) * HD ** (-0.5)
            turned_k = jnp.concatenate(to_k, axis=-1) * HD ** (-0.5)
            grad_v = jnp.concatenate(to_v, axis=-1).astype(LOW)
            cosine, sine = unfold_turn(turns[rows, cols])
            lane = lax.broadcasted_iota(jnp.int32, (1, 2 * HD), 1)
            sign = jnp.where(jnp.bitwise_and(lane, HD - 1) < HD // 2, -1.0, 1.0)
            swing = sign * (
                turned_q * partner(query.astype(F32)) + turned_k * partner(key.astype(F32))
            )
            for n, place_at in enumerate((row_at, col_at)):
                vec_g[FREQ_ROW + n, :, cols] += jnp.sum(swing * place_at, axis=0, keepdims=True)
            grad_q = (turned_q * cosine - partner(turned_q) * sine).astype(LOW)
            grad_k = (turned_k * cosine - partner(turned_k) * sine).astype(LOW)
            for where, low in ((cols, grad_q), (key_cols, grad_k), (value_cols, grad_v)):
                qkv[rows, where] = low
                add_row(qkv_bg, where, low)

        loop(H // 2, heads)

        def normed_tile(t):
            cols = span(t * TILE, TILE)
            wide[:, cols] = dot_nt(qkv[rows, :], qkv_w[cols, :])

        loop(D // TILE, normed_tile)

        def source_back(here, inside):
            part, hat = norm_back(xin[here, :].astype(F32), GAIN_ONE, wide[inside, :])
            grad_in = mid[here, :] + part
            mid[here, :] = grad_in
            xin[here, :] = (hat * vector(GAIN_ONE) + vector(SHIFT_ONE)).astype(LOW)
            shipped[here, :] = grad_in.astype(LOW)

        chunks(b, source_back)

        @pl.when(at.role > 0)
        def _():
            pipe(1, b, gin, at.role - 1).start()

        ship_start(1, b, mid, grad_out_ref)

    loop(images_here, backward)

    def to_sibling(n, slot):
        k, other = slot % 2, slot < 2
        group = 2 * (1 - at.core + 2 * k) + (1 - at.y if other else at.y)
        return remote(
            block_of(partials[n], group), firsts[n].at[slot],
            reduce_send.at[n, slot], reduce_arrive.at[n, slot], at.sibling(),
        )

    def held(n, slot):
        k, other = slot % 2, slot < 2
        return 2 * (at.core + 2 * k) + (1 - at.y if other else at.y)

    def to_across(n, k):
        return remote(
            block_of(partials[n], held(n, k)), seconds[n].at[k],
            reduce_send.at[n, 4 + k], reduce_arrive.at[n, 4 + k], at.across(),
        )

    def to_owner(n, k):
        return remote(
            block_of(partials[n], held(n, 2 + k)), thirds[n].at[at.half],
            reduce_send.at[n, 6 + k], reduce_arrive.at[n, 6 + at.half], at.along(k),
        )

    def from_other(n, k):
        return remote(
            block_of(partials[n], held(n, 2 + k)), thirds[n].at[k],
            reduce_send.at[n, 6 + k], reduce_arrive.at[n, 6 + k], at.along(k),
        )

    def add(n, slot, sources, index):
        ref = partials[n]
        size = ref.shape[0] // GROUPS
        base = held(n, slot) * size
        step = 16

        def body(i):
            here = pl.ds(pl.multiple_of(base + i * step, step), step)
            there = span(i * step, step)
            total = ref[here, :].astype(F32)
            for source in sources:
                total = total + source[index, there, :].astype(F32)
            ref[here, :] = total.astype(ref.dtype)

        loop(size // step, body)

    def reduce_start(n):
        for slot in range(4):
            to_sibling(n, slot).start()

    def reduce_across(n):
        for k in range(2):
            to_sibling(n, k).wait_recv()
            add(n, k, [firsts[n]], k)
            to_across(n, k).start()
        for k in range(2):
            to_sibling(n, 2 + k).wait_recv()
            add(n, 2 + k, [firsts[n]], 2 + k)

    def reduce_along(n):
        for k in range(2):
            to_across(n, k).wait_recv()
            add(n, 2 + k, [seconds[n]], k)

            @pl.when(jnp.logical_not(at.is_self(k)))
            def _():
                to_owner(n, k).start()

    def down_tile(t):
        cols = span(t * TILE, TILE)
        down_w[cols, :] = dot_tn(act[:, cols], gin[...]).astype(LOW)

    loop(down_w.shape[0] // TILE, down_tile)
    reduce_start(4)

    def up_tile(t):
        cols = span(t * TILE, TILE)
        up_w[:, cols] = dot_tn(n2[...], slope[:, cols]).astype(LOW)

    loop(up_w.shape[1] // TILE, up_tile)
    reduce_start(3)
    reduce_across(4)

    def proj_tile(t):
        cols = span(t * TILE, TILE)
        proj_w[:, cols] = dot_tn(att[...], g1[:, cols]).astype(LOW)

    loop(D // TILE, proj_tile)
    reduce_start(2)

    def qkv_tile(t):
        cols = span(t * TILE, TILE)
        qkv_w[:, cols] = dot_tn(xin[...], qkv[:, cols]).astype(LOW)

    loop(qkv_w.shape[1] // TILE, qkv_tile)
    reduce_start(1)
    reduce_across(3)

    small_f[...] = jnp.zeros_like(small_f)

    def give_vector(row):
        small_f[...] += fold(vec_g[row], q, row, plain)

    def give_frequency(t):
        small_f[...] += fold(vec_g[FREQ_ROW + t], q, FREQ_ROW, apart + as_float(t) * (D // 2))

    def give_qkv(t):
        small_f[...] += fold(qkv_bg[:, span(t * D, D)], 3 * q, 7, plain + as_float(t) * D)

    def give_up(t):
        small_f[...] += fold(up_bg[:, span(t * D, D)], 4 * q, 10, plain + as_float(t) * D)

    loop(FREQ_ROW, give_vector)
    loop(2, give_frequency)
    loop(3, give_qkv)
    loop(4, give_up)
    reduce_start(0)

    reduce_along(4)
    reduce_across(2)
    reduce_across(1)
    reduce_across(0)
    for n in (3, 2, 1, 0):
        reduce_along(n)

    used = [0]

    def tile_copy(slot, target):
        return pltpu.make_async_copy(
            stage.at[pl.ds(slot * q, q), :], target, tile_sem.at[slot]
        )

    pending = [None] * 4

    def total(n, row, col, size, width, target):
        slot = used[0] % 4
        used[0] += 1
        if pending[slot] is not None:
            tile_copy(slot, pending[slot]).wait()
        base = held(n, 2)

        def run(pick):
            step = 16

            def body(i):
                there = pl.ds(pl.multiple_of(row + i * step, step), step)
                low, high = pick(there, i * step)
                stage[pl.ds(pl.multiple_of(slot * q + i * step, step), step), :] = low.astype(F32) + high.astype(F32)

            loop(size // step, body)

        cols = pl.ds(col, width)

        def mine(k):
            start = held(n, 2 + k) * (partials[n].shape[0] // GROUPS) + row

            def read(offset):
                return partials[n][pl.ds(pl.multiple_of(start + offset, 16), 16), cols]

            return read

        @pl.when(at.away)
        def _():
            run(lambda there, offset: (thirds[n][0, there, cols], thirds[n][1, there, cols]))

        @pl.when(at.is_self(0))
        def _():
            run(lambda there, offset: (mine(0)(offset), thirds[n][1, there, cols]))

        @pl.when(at.is_self(1))
        def _():
            run(lambda there, offset: (thirds[n][0, there, cols], mine(1)(offset)))

        tile_copy(slot, target).start()
        pending[slot] = target

    def total_wait(n):
        for k in range(2):

            @pl.when(jnp.logical_not(at.is_self(k)))
            def _():
                from_other(n, k).wait_recv()

    for n in (4, 3, 2, 1):
        total_wait(n)
        size, width = totals[n].shape
        for row in range(0, size, q):
            for col in range(0, width, D):
                target = totals[n].at[pl.ds(row, q), pl.ds(col, D)]
                total(n, row, col, q, D, target)
    total_wait(0)

    @pl.when(at.away)
    def _():
        totals[0][...] = third_4[0] + third_4[1]

    for k in range(2):

        @pl.when(at.is_self(k))
        def _():
            totals[0][...] = third_4[1 - k] + small_f[span(held(0, 2 + k) * SMALL_ROWS, SMALL_ROWS), :]

    for slot, target in enumerate(pending):
        if target is not None:
            tile_copy(slot, target).wait()

    for b in range(images_here):
        ship_wait(1, b, mid, grad_out_ref)

        @pl.when(at.role > 0)
        def _():
            pipe(1, b, gin, at.role - 1).wait_send()

    for n in range(5):
        for slot in range(4):
            to_sibling(n, slot).wait_send()
        for k in range(2):
            to_across(n, k).wait_send()

            @pl.when(jnp.logical_not(at.is_self(k)))
            def _():
                to_owner(n, k).wait_send()


def run_block(replicas, sections, parts, images, cotangent, facts_col, facts_row):
    images_here, patches = images.shape[:2]
    rows = images_here * patches
    hidden = parts[2].shape[1]
    anywhere = pl.BlockSpec(memory_space=pl.ANY)
    flat = [value.reshape(-1, value.shape[-1]) for value in (images, cotangent, facts_col, facts_row)]
    shapes = [part.shape for part in parts]
    outs = [jax.ShapeDtypeStruct((rows, D), F32)] * 2
    outs += [jax.ShapeDtypeStruct(shape, F32) for shape in shapes]
    vmem, dma = pltpu.VMEM, pltpu.SemaphoreType.DMA
    kinds = [part.dtype for part in parts[:4]] + [F32]

    def buffers(slots):
        return [vmem((slots, *shape), kind) for shape, kind in zip(shapes, kinds)]

    scratch = [vmem((GROUPS * shape[0], shape[1]), LOW) for shape in shapes]
    scratch += buffers(4) + buffers(2) + buffers(2)
    scratch += [
        vmem((rows, D), LOW),
        vmem((rows, D), LOW),
        vmem((rows, LANES), LOW),
        vmem((images_here * 8, patches), F32),
        vmem((rows, 3 * D), LOW),
        vmem((images_here * H, patches, patches), LOW),
        vmem((rows, D), LOW),
        vmem((rows, D), F32),
        vmem((rows, D), LOW),
        vmem((rows, hidden), LOW),
        vmem((rows, hidden), LOW),
        vmem((rows, D), LOW),
        vmem((patches, D), F32),
        vmem((rows, D), LOW),
        vmem((rows, D), F32),
        vmem((rows, D), F32),
        vmem((8, 1, D), F32),
        vmem((1, 3 * D), F32),
        vmem((1, hidden), F32),
        vmem((8, 1, D), F32),
        vmem((1, 3 * D), F32),
        vmem((1, hidden), F32),
        vmem((GROUPS * SMALL_ROWS, LANES), F32),
        dma((5, 8)),
        dma((5, GROUPS)),
        dma((5, 8)),
        dma((5, 8)),
        dma((4,)),
        dma((4,)),
        dma((2, images_here)),
        dma((2, images_here)),
        dma((2, images_here)),
        dma((2, images_here)),
        dma((4,)),
    ]
    results = pl.pallas_call(
        functools.partial(block_kernel, replicas, sections, images_here, patches),
        out_shape=outs,
        in_specs=[anywhere] * 9,
        out_specs=[anywhere] * 6 + [pl.BlockSpec(memory_space=vmem)],
        scratch_shapes=scratch,
        compiler_params=pltpu.CompilerParams(
            collective_id=0, has_side_effects=True, vmem_limit_bytes=63 * 1024 * 1024
        ),
        name="block",
    )(*parts, *flat)
    outputs, input_grads = (value.reshape(images.shape) for value in results[:2])
    return outputs, input_grads, results[2:]


def rows_from(vector):
    short = -vector.shape[0] % LANES
    return jnp.pad(vector, (0, short)).reshape(-1, LANES)


def pack(vectors):
    block = jnp.concatenate([rows_from(vector) for vector in vectors], axis=0)
    return jnp.pad(block, ((0, SMALL_ROWS - block.shape[0]), (0, 0)))


def unpack(block, sizes):
    found, start = [], 0
    for size in sizes:
        count = -(-size // LANES)
        found.append(block[start : start + count].reshape(-1)[:size])
        start += count
    return found


MATRICES = (2, 4, 8, 10)
VECTORS = (0, 1, 5, 6, 7, 11, 12, 3, 9)


def local(images, cotangent, kept_count, kept_index, *weights):
    sections = lax.axis_size("section")
    replicas = lax.axis_size("dp") // GROUPS
    subgroups = [[g * replicas + r for r in range(replicas)] for g in range(GROUPS)]
    if replicas > 1:
        weights = tuple(
            lax.all_gather(value, "dp", axis=1, tiled=True, axis_index_groups=subgroups)
            for value in weights
        )
    weights = tuple(value[0] for value in weights)
    sizes = [weights[n].shape[0] for n in VECTORS]
    patches = images.shape[1]
    keep = (jnp.arange(patches)[None, :] < kept_count[:, None]).astype(jnp.int32)
    facts = jnp.stack([keep, kept_index // GRID, kept_index % GRID], axis=1).astype(F32)
    facts_row = jnp.pad(facts, ((0, 0), (0, 5), (0, 0)))
    facts_col = jnp.pad(jnp.swapaxes(facts, 1, 2), ((0, 0), (0, 0), (0, LANES - 3))).astype(LOW)
    parts = [weights[n] for n in MATRICES] + [pack([weights[n] for n in VECTORS])]
    outputs, input_grads, sums = run_block(
        replicas, sections, parts, images, cotangent, facts_col, facts_row
    )
    grads = [None] * len(weights)
    for n, value in zip(MATRICES, sums):
        grads[n] = value
    for n, vector in zip(VECTORS, unpack(sums[-1], sizes)):
        grads[n] = vector
    if replicas > 1:
        grads = [
            lax.psum_scatter(
                value, "dp", scatter_dimension=0, tiled=True, axis_index_groups=subgroups
            )
            for value in grads
        ]
    return (outputs[None], input_grads[None], *(value[None] for value in grads))


def solution(mesh):
    in_specs = (
        P("dp", None, None),
        P("dp", None, None),
        P("dp"),
        P("dp", None),
        P("section", "dp"),
        P("section", "dp"),
        P("section", "dp", None),
        P("section", "dp"),
        P("section", "dp", None),
        P("section", "dp"),
        P("section", "dp"),
        P("section", "dp"),
        P("section", "dp", None),
        P("section", "dp"),
        P("section", "dp", None),
        P("section", "dp"),
        P("section", "dp"),
    )
    out_specs = (
        P("section", "dp", None, None),
        P("section", "dp", None, None),
        P("section", "dp"),
        P("section", "dp"),
        P("section", "dp", None),
        P("section", "dp"),
        P("section", "dp", None),
        P("section", "dp"),
        P("section", "dp"),
        P("section", "dp"),
        P("section", "dp", None),
        P("section", "dp"),
        P("section", "dp", None),
        P("section", "dp"),
        P("section", "dp"),
    )
    return jax.shard_map(local, mesh=mesh, in_specs=in_specs, out_specs=out_specs, check_vma=False)
```

time: 1770 us -> 481 us (0.27)
  waiting for transfers between devices: 1160 us -> 0 us
  Pallas kernels: 0 us -> 457 us
  matrix products: 312 us -> 0 us
  other arithmetic: 103 us -> 2.83 us
  local copies, waits for them, and re-layouts: 87.4 us -> 16.7 us
  blocking collectives: 50.5 us -> 0 us
  starting transfers between devices: 28.9 us -> 0 us
  between operations: 20.6 us -> 0.68 us
    reduce_scatter x4 -> x0, waiting for transfers between devices: 538 us -> none  [the longest x1 167 us: local(): lax.psum_scatter(totals[10][None], 'dp', scatter_dimension=1, tiled=True)]
    pallas_call x0 -> x1, Pallas kernels: none -> 457 us  [run_block(): pl.pallas_call(functools.partial(block_kernel, replicas, sections, images...]
    unnamed x26 -> x0, waiting for transfers between devices: 418 us -> none
    dot_general x90 -> x0, matrix products: 312 us -> none  [the longest x5 56.9 us: forward_block(): jnp.dot(normed_two, up_matrix, preferred_element_type=jnp.float32)]
    all_gather x4 -> x0, waiting for transfers between devices: 179 us -> none  [the longest x1 79.2 us: local(): lax.all_gather(up_matrix, 'dp', axis=1, tiled=True)]
    reduce_sum x59 -> x0, other arithmetic: 56.5 us -> none  [the longest x15 17.4 us: layer_norm(): return centred * lax.rsqrt(variance + EPSILON) * gain_vector + shift_vector]
    unnamed x685 -> x20, local copies, waits for them, and re-layouts: 56.2 us -> 9.9 us
    ppermute x8 -> x0, starting transfers between devices: 27.4 us -> none  [shifted(): lax.ppermute(value, axis, [(source, source + steps) for source in range(f...]
  transfers between devices with their start and end apart: 25 -> 0, of which waited for: 19 -> 0; matrix products, arithmetic and copies ran while one was open for 13% -> 0% of each run, Pallas kernels for 0% -> 0%
where the time goes in v2:
time: 481 us; the launch traced here: 477 us
  Pallas kernels  457 us (95%)
  local copies, waits for them, and re-layouts  16.7 us (3%)
    pallas_call x1, Pallas kernels, run_block(): pl.pallas_call(functools.partial(block_kernel, replicas, sections, images...  457 us
    unnamed x20, local copies, waits for them, and re-layouts  9.9 us

profile of v2, /device:TPU:17, one launch (start us, length us, event | category | flops | bytes accessed | tf_op | source)
XLA Modules:
  0.0 476.9 jit_solution(3127451459984143884)
XLA Ops:
  0.6 0.7 pad_bitcast_fusion.2
  1.3 0.7 pad_bitcast_fusion.4
  2.0 0.7 pad_bitcast_fusion.6
  2.7 0.7 reduce
  3.4 0.7 reduce.1
  4.1 0.7 pad_bitcast_fusion.8
  4.7 0.1 concatenate.3
  4.9 0.6 pad.47.refs_4_
  5.5 0.7 fusion.1
  6.2 0.7 compare_convert_fusion
  6.9 0.2 copy.34
  7.1 0.7 pad.48.clone
  7.8 0.6 pad_bitcast_fusion.refs_8_
  8.4 456.7 %block.1 = (f32[512,768]{1,0:T(8,128)}, f32[512,768]{1,0:T(8,128)}, f32[96,2304]{1,0:T(8,128)}, f32[96,768]{1,0:T(8,128)}, f32[96,3072]{1,0:T(8,128)}, /*index=5*/f32[384,768]{1,0:T(8,128)}, f32[16,128]{1,0:T(8,128)}) custom-call(bf16[96,2304]{1,0:T(8,128)(2,1)} %bitcast.64, bf16[96,768]{1,0:T(8,128)(2,1)} %bitcast.66, bf16[96,3072]{1,0:T(8,128)(2,1)} %bitcast.61, ...), custom_call_target="tpu_custom_call" | custom-call | tf_op jit(solution)/shard_map/block/pallas_call | solution.py:966
  465.2 1.5 fusion.2
  466.6 0.8 slice_bitcast_fusion
  467.4 0.6 copy.38
  468.0 0.6 broadcast_in_dim.11
  468.5 0.0 copy-start
  468.6 2.8 copy.45
  471.3 0.0 copy-done
  471.3 0.0 copy-start.3
  471.3 1.1 copy.46
  472.5 0.6 copy-done.3
  473.1 0.0 copy-start.4
  473.1 0.0 copy-start.2
  473.1 0.9 copy.47
  474.0 0.2 copy-done.4
  474.2 0.0 copy-start.1
  474.2 0.7 copy.48
  474.9 0.0 copy-done.2
  474.9 1.0 copy.49
  475.9 0.0 copy-done.1
  475.9 1.0 copy.50
  (3 shorter events, 0.0 us)
Async XLA Ops:
  468.5 2.8 copy-start
  471.3 1.7 copy-start.3
  473.1 1.1 copy-start.4
  473.1 1.8 copy-start.2
  474.2 1.7 copy-start.1

commit v3 on v2

--- a/solution.py
+++ b/solution.py
@@ -16,8 +16,9 @@
 MASKED = -1e30
 GROUPS = 8
 LANES = 128
-TILE = 256
+TILE = 768
 CHUNK = 64
+GRAD_TILE = 768
 MESH = pl.DeviceIdType.MESH
 F32 = jnp.float32
 LOW = jnp.bfloat16
@@ -114,12 +115,12 @@
     return lax.dot_general(a, b, (((0,), (0,)), ((), ())), preferred_element_type=F32)
 
 
-def loop(count, body):
+def loop(count, body, unroll=1):
     def step(i, carry):
         body(i)
         return carry
 
-    lax.fori_loop(0, count, step, 0)
+    lax.fori_loop(0, count, step, 0, unroll=unroll)
 
 
 SMALL_ROWS = 16
@@ -149,9 +150,18 @@
 
 def spread_positions():
     at = positions(D)
-    head = quotient(at, HD)
-    inside = at - head * HD
-    return head * (HD // 2) + inside - quotient(inside, HD // 2) * (HD // 2)
+    pair = quotient(at, 2 * HD)
+    return at - quotient(at, HD) * HD + pair * HD
+
+
+def paired_positions():
+    at = positions(D)
+    pair = quotient(at, 2 * HD)
+    inside = at - pair * (2 * HD)
+    half = quotient(inside, HD)
+    rest = inside - half * HD
+    head = quotient(rest, HD // 2)
+    return pair * (2 * HD) + head * HD + half * (HD // 2) + rest - head * (HD // 2)
 
 
 def expand(block, size, first_row, index):
@@ -179,14 +189,20 @@
     return centred * scale, scale
 
 
+def lanes_of(shape):
+    return lax.broadcasted_iota(jnp.int32, shape, 1)
+
+
 def first_half(shape):
-    return jnp.bitwise_and(lax.broadcasted_iota(jnp.int32, shape, 1), HD - 1) < HD // 2
+    return jnp.bitwise_and(lanes_of(shape), 2 * HD - 1) < HD
 
 
 def partner(values):
-    left = pltpu.roll(values, values.shape[1] - HD // 2, 1)
-    right = pltpu.roll(values, HD // 2, 1)
-    return jnp.where(first_half(values.shape), left, right)
+    pieces = [
+        pltpu.roll(values[:, start : start + 2 * HD], HD, 1)
+        for start in range(0, values.shape[1], 2 * HD)
+    ]
+    return jnp.concatenate(pieces, axis=1) if len(pieces) > 1 else pieces[0]
 
 
 def unfold_turn(table):
@@ -194,9 +210,12 @@
     return jnp.where(first, table, other), jnp.where(first, -other, table)
 
 
+LOG2_E = 1.0 / math.log(2.0)
+
+
 def gelu_pair(u):
     phi = 0.5 * (1.0 + lax.erf(u * math.sqrt(0.5)))
-    density = jnp.exp(-0.5 * u * u) * (1.0 / math.sqrt(2.0 * math.pi))
+    density = jnp.exp2(u * u * (-0.5 * LOG2_E)) * (1.0 / math.sqrt(2.0 * math.pi))
     return u * phi, phi + u * density
 
 
@@ -366,6 +385,10 @@
     q = D // GROUPS
     plain = positions(D)
     apart = spread_positions()
+    paired = paired_positions()
+
+    def qkv_positions(t):
+        return jnp.where(t < 2, paired, plain) + as_float(t) * D
 
     def take_vector(row):
         vec[row] = expand(block, q, row, plain)
@@ -374,7 +397,7 @@
         vec[FREQ_ROW + t] = expand(block, q, FREQ_ROW, apart + as_float(t) * (D // 2))
 
     def take_qkv(t):
-        qkv_b[:, span(t * D, D)] = expand(block, 3 * q, 7, plain + as_float(t) * D)
+        qkv_b[:, span(t * D, D)] = expand(block, 3 * q, 7, qkv_positions(t))
 
     def take_up(t):
         up_b[:, span(t * D, D)] = expand(block, 4 * q, 10, plain + as_float(t) * D)
@@ -460,7 +483,16 @@
         loop(
             patches // CHUNK,
             lambda i: body(span(b * patches + i * CHUNK, CHUNK), span(i * CHUNK, CHUNK)),
-        )
+            unroll=patches // CHUNK,
+        )
+
+    def own_lanes(e):
+        inside = jnp.bitwise_and(lanes_of((patches, 2 * HD)), HD - 1) < HD // 2
+        return inside if e == 0 else jnp.logical_not(inside)
+
+    def value_lanes(e):
+        inside = lanes_of((patches, 2 * HD)) < HD
+        return inside if e == 0 else jnp.logical_not(inside)
 
     def forward(b):
         rows = span(b * patches, patches)
@@ -470,7 +502,7 @@
             pipe(0, b, xin, at.role - 1).wait_recv()
 
         keep_col = fcol[rows, :].astype(F32)[:, 0:1]
-        keep_row = frow[span(b * 8, 8), :][0:1, :]
+        barred = jnp.where(frow[span(b * 8, 8), :][0:1, :] > 0, 0.0, MASKED)
 
         def norm_one(here, inside):
             hat, _ = normalise(xin[here, :].astype(F32))
@@ -486,7 +518,7 @@
             turned = raw * cosine + partner(raw) * sine
             qkv[rows, cols] = turned.astype(LOW)
 
-        loop(2 * D // TILE, turn)
+        loop(2 * D // TILE, turn, unroll=2)
 
         def plain_values(t):
             cols = span(t * TILE + 2 * D, TILE)
@@ -499,19 +531,21 @@
             query = qkv[rows, cols]
             key = qkv[rows, span(D + pair * 2 * HD, 2 * HD)]
             value = qkv[rows, span(2 * D + pair * 2 * HD, 2 * HD)]
+            value = jnp.concatenate([value, jnp.ones_like(value)], axis=1)
             found = []
             for e in range(2):
-                inside = slice(e * HD, (e + 1) * HD)
-                scores = dot_nt(query[:, inside], key[:, inside]) * HD ** (-0.5)
-                scores = jnp.where(keep_row > 0, scores, MASKED)
-                powers = jnp.exp(scores - jnp.max(scores, axis=-1, keepdims=True))
-                share = 1.0 / jnp.sum(powers, axis=-1, keepdims=True)
-                soft = (powers * share).astype(LOW)
-                probs[b * H + 2 * pair + e] = soft
-                found.append(dot(soft, value[:, inside]))
-            att[rows, cols] = jnp.concatenate(found, axis=-1).astype(LOW)
-
-        loop(H // 2, heads)
+                own_query = jnp.where(own_lanes(e), query, jnp.zeros_like(query))
+                scores = dot_nt(own_query, key) * (HD ** (-0.5) * LOG2_E) + barred
+                powers = jnp.exp2(scores - jnp.max(scores, axis=1, keepdims=True))
+                both = dot(powers.astype(LOW), value)
+                share = 1.0 / both[:, 2 * HD :]
+                probs[b * H + 2 * pair + e] = (
+                    powers * jnp.concatenate([share] * (patches // (2 * HD)), axis=1)
+                ).astype(LOW)
+                found.append(both[:, : 2 * HD] * share)
+            att[rows, cols] = jnp.where(value_lanes(0), found[0], found[1]).astype(LOW)
+
+        loop(H // 2, heads, unroll=H // 2)
 
         def project(t):
             cols = span(t * TILE, TILE)
@@ -526,14 +560,10 @@
 
         chunks(b, norm_two)
 
-        def raise_tile(t):
-            cols = span(t * TILE, TILE)
-            hidden = dot(n2[rows, :], up_w[:, cols]) + up_b[:, cols]
-            value, gradient = gelu_pair(hidden)
-            act[rows, cols] = value.astype(LOW)
-            slope[rows, cols] = gradient.astype(LOW)
-
-        loop(up_w.shape[1] // TILE, raise_tile)
+        hidden = dot(n2[rows, :], up_w[...]) + up_b[...]
+        value, gradient = gelu_pair(hidden)
+        act[rows, :] = value.astype(LOW)
+        slope[rows, :] = gradient.astype(LOW)
 
         def lower_tile(t):
             cols = span(t * TILE, TILE)
@@ -596,14 +626,10 @@
 
         chunks(b, mask_coming)
 
-        def hidden_tile(t):
-            cols = span(t * TILE, TILE)
-            grad = dot_nt(gin[rows, :], down_w[cols, :])
-            low = (grad * slope[rows, cols].astype(F32)).astype(LOW)
-            slope[rows, cols] = low
-            add_row(up_bg, cols, low)
-
-        loop(up_w.shape[1] // TILE, hidden_tile)
+        grad = dot_nt(gin[rows, :], down_w[...])
+        low = (grad * slope[rows, :].astype(F32)).astype(LOW)
+        slope[rows, :] = low
+        up_bg[...] += jnp.sum(low.astype(F32), axis=0, keepdims=True)
 
         def normed_two_tile(t):
             cols = span(t * TILE, TILE)
@@ -635,33 +661,32 @@
             grad = shipped[rows, cols]
             to_q, to_k, to_v = [], [], []
             for e in range(2):
-                inside = slice(e * HD, (e + 1) * HD)
+                own_grad = jnp.where(value_lanes(e), grad, jnp.zeros_like(grad))
                 soft_low = probs[b * H + 2 * pair + e]
                 soft = soft_low.astype(F32)
-                grad_soft = dot_nt(grad[:, inside], value[:, inside])
-                centre = jnp.sum(soft * grad_soft, axis=-1, keepdims=True)
+                grad_soft = dot_nt(own_grad, value)
+                centre = jnp.sum(soft * grad_soft, axis=1, keepdims=True)
                 grad_scores = (soft * (grad_soft - centre)).astype(LOW)
-                to_v.append(dot_tn(soft_low, grad[:, inside]))
-                to_q.append(dot(grad_scores, key[:, inside]))
-                to_k.append(dot_tn(grad_scores, query[:, inside]))
-            turned_q = jnp.concatenate(to_q, axis=-1) * HD ** (-0.5)
-            turned_k = jnp.concatenate(to_k, axis=-1) * HD ** (-0.5)
-            grad_v = jnp.concatenate(to_v, axis=-1).astype(LOW)
+                to_q.append(dot(grad_scores, key))
+                to_k.append(dot_tn(grad_scores, query))
+                to_v.append(dot_tn(soft_low, grad))
+            scale = HD ** (-0.5)
+            turned_q = jnp.where(own_lanes(0), to_q[0], to_q[1]) * scale
+            turned_k = jnp.where(own_lanes(0), to_k[0], to_k[1]) * scale
+            grad_v = jnp.where(value_lanes(0), to_v[0], to_v[1]).astype(LOW)
             cosine, sine = unfold_turn(turns[rows, cols])
-            lane = lax.broadcasted_iota(jnp.int32, (1, 2 * HD), 1)
-            sign = jnp.where(jnp.bitwise_and(lane, HD - 1) < HD // 2, -1.0, 1.0)
-            swing = sign * (
-                turned_q * partner(query.astype(F32)) + turned_k * partner(key.astype(F32))
-            )
+            other_q, other_k = partner(turned_q), partner(turned_k)
+            sign = jnp.where(first_half((1, 2 * HD)), 1.0, -1.0)
+            swing = sign * (other_q * query.astype(F32) + other_k * key.astype(F32))
             for n, place_at in enumerate((row_at, col_at)):
                 vec_g[FREQ_ROW + n, :, cols] += jnp.sum(swing * place_at, axis=0, keepdims=True)
-            grad_q = (turned_q * cosine - partner(turned_q) * sine).astype(LOW)
-            grad_k = (turned_k * cosine - partner(turned_k) * sine).astype(LOW)
+            grad_q = (turned_q * cosine - other_q * sine).astype(LOW)
+            grad_k = (turned_k * cosine - other_k * sine).astype(LOW)
             for where, low in ((cols, grad_q), (key_cols, grad_k), (value_cols, grad_v)):
                 qkv[rows, where] = low
                 add_row(qkv_bg, where, low)
 
-        loop(H // 2, heads)
+        loop(H // 2, heads, unroll=H // 2)
 
         def normed_tile(t):
             cols = span(t * TILE, TILE)
@@ -755,32 +780,27 @@
                 to_owner(n, k).start()
 
     def down_tile(t):
-        cols = span(t * TILE, TILE)
+        cols = span(t * GRAD_TILE, GRAD_TILE)
         down_w[cols, :] = dot_tn(act[:, cols], gin[...]).astype(LOW)
 
-    loop(down_w.shape[0] // TILE, down_tile)
+    loop(down_w.shape[0] // GRAD_TILE, down_tile)
     reduce_start(4)
 
     def up_tile(t):
-        cols = span(t * TILE, TILE)
+        cols = span(t * GRAD_TILE, GRAD_TILE)
         up_w[:, cols] = dot_tn(n2[...], slope[:, cols]).astype(LOW)
 
-    loop(up_w.shape[1] // TILE, up_tile)
+    loop(up_w.shape[1] // GRAD_TILE, up_tile)
     reduce_start(3)
     reduce_across(4)
-
-    def proj_tile(t):
-        cols = span(t * TILE, TILE)
-        proj_w[:, cols] = dot_tn(att[...], g1[:, cols]).astype(LOW)
-
-    loop(D // TILE, proj_tile)
+    proj_w[...] = dot_tn(att[...], g1[...]).astype(LOW)
     reduce_start(2)
 
     def qkv_tile(t):
-        cols = span(t * TILE, TILE)
+        cols = span(t * D, D)
         qkv_w[:, cols] = dot_tn(xin[...], qkv[:, cols]).astype(LOW)
 
-    loop(qkv_w.shape[1] // TILE, qkv_tile)
+    loop(qkv_w.shape[1] // D, qkv_tile)
     reduce_start(1)
     reduce_across(3)
 
@@ -793,7 +813,7 @@
         small_f[...] += fold(vec_g[FREQ_ROW + t], q, FREQ_ROW, apart + as_float(t) * (D // 2))
 
     def give_qkv(t):
-        small_f[...] += fold(qkv_bg[:, span(t * D, D)], 3 * q, 7, plain + as_float(t) * D)
+        small_f[...] += fold(qkv_bg[:, span(t * D, D)], 3 * q, 7, qkv_positions(t))
 
     def give_up(t):
         small_f[...] += fold(up_bg[:, span(t * D, D)], 4 * q, 10, plain + as_float(t) * D)
@@ -1001,6 +1021,13 @@
 VECTORS = (0, 1, 5, 6, 7, 11, 12, 3, 9)
 
 
+def pair_heads(matrix):
+    rows = matrix.shape[0]
+    split = matrix[:, : 2 * D].reshape(rows, H, 2, 2, HD // 2)
+    turned = jnp.swapaxes(split, 2, 3).reshape(rows, 2 * D)
+    return jnp.concatenate([turned, matrix[:, 2 * D :]], axis=1)
+
+
 def local(images, cotangent, kept_count, kept_index, *weights):
     sections = lax.axis_size("section")
     replicas = lax.axis_size("dp") // GROUPS
@@ -1017,13 +1044,14 @@
     facts = jnp.stack([keep, kept_index // GRID, kept_index % GRID], axis=1).astype(F32)
     facts_row = jnp.pad(facts, ((0, 0), (0, 5), (0, 0)))
     facts_col = jnp.pad(jnp.swapaxes(facts, 1, 2), ((0, 0), (0, 0), (0, LANES - 3))).astype(LOW)
-    parts = [weights[n] for n in MATRICES] + [pack([weights[n] for n in VECTORS])]
+    parts = [pair_heads(weights[2])] + [weights[n] for n in MATRICES[1:]] + [pack([weights[n] for n in VECTORS])]
     outputs, input_grads, sums = run_block(
         replicas, sections, parts, images, cotangent, facts_col, facts_row
     )
     grads = [None] * len(weights)
     for n, value in zip(MATRICES, sums):
         grads[n] = value
+    grads[2] = pair_heads(grads[2])
     for n, vector in zip(VECTORS, unpack(sums[-1], sizes)):
         grads[n] = vector
     if replicas > 1:

time: 481 us -> 405 us (0.84)
  Pallas kernels: 457 us -> 378 us
    pallas_call x1, Pallas kernels: 457 us -> 378 us  [run_block(): pl.pallas_call(functools.partial(block_kernel, replicas, sections, images...]
where the time goes in v3:
time: 405 us; the launch traced here: 404 us
  Pallas kernels  378 us (93%)
  local copies, waits for them, and re-layouts  21.5 us (5%)
    pallas_call x1, Pallas kernels, run_block(): pl.pallas_call(functools.partial(block_kernel, replicas, sections, images...  378 us
    unnamed x20, local copies, waits for them, and re-layouts  9.75 us

profile of v3, /device:TPU:17, one launch (start us, length us, event | category | flops | bytes accessed | tf_op | source)
XLA Modules:
  0.0 404.3 jit_solution(3335496331461214587)
XLA Ops:
  0.6 0.7 pad_bitcast_fusion.8
  1.3 0.7 reduce
  2.0 0.7 reduce.1
  2.7 0.7 pad_bitcast_fusion.6
  3.4 0.7 pad_bitcast_fusion.4
  4.1 0.7 pad_bitcast_fusion.2
  4.7 0.1 concatenate.10
  4.9 0.6 pad.47.refs_4_
  5.5 0.7 compare_convert_fusion
  6.2 0.7 fusion.1
  6.9 0.6 pad_bitcast_fusion.refs_8_
  7.5 0.2 copy.45
  7.7 0.7 pad.48.clone
  8.4 0.9 slice.78
  9.3 1.0 slice.77
  10.3 0.2 copy.36
  10.6 0.2 copy.38
  10.8 0.8 pad_maximum_fusion.refs_0_
  11.6 378.4 %block.1 = (f32[512,768]{1,0:T(8,128)}, f32[512,768]{1,0:T(8,128)}, f32[96,2304]{1,0:T(8,128)}, f32[96,768]{1,0:T(8,128)}, f32[96,3072]{1,0:T(8,128)}, /*index=5*/f32[384,768]{1,0:T(8,128)}, f32[16,128]{1,0:T(8,128)}) custom-call(bf16[96,2304]{1,0:T(8,128)(2,1)} %pad_maximum_fusion.refs_0_, bf16[96,768]{1,0:T(8,128)(2,1)} %bitcast.79, ...), custom_call_target="tpu_custom_call" | custom-call | tf_op jit(solution)/shard_map/block/pallas_call | solution.py:986
  389.9 1.5 fusion.2
  391.4 0.8 slice_bitcast_fusion
  392.2 0.6 copy.49
  392.8 0.6 broadcast_in_dim.11
  393.3 1.0 slice.68
  394.3 1.1 slice.67
  395.4 0.2 copy.43
  395.6 0.3 copy.41
  395.9 0.1 copy.42
  395.9 0.1 maximum_bitcast_fusion
  396.0 0.0 copy-start.1
  396.0 1.3 copy.44
  397.3 0.3 copy-done.1
  397.6 0.0 copy-start
  397.6 1.1 copy.55
  398.8 0.8 copy-done
  399.6 0.0 copy-start.4
  399.6 0.0 copy-start.3
  399.6 1.1 copy.56
  400.8 0.0 copy-done.4
  400.8 0.7 copy.57
  401.5 0.1 copy-done.3
  401.6 0.0 copy-start.2
  401.6 1.0 copy.58
  402.6 0.7 copy-done.2
  403.3 1.0 copy.59
  (4 shorter events, 0.1 us)
Async XLA Ops:
  396.0 1.6 copy-start.1
  397.6 2.0 copy-start
  399.6 1.1 copy-start.4
  399.6 1.9 copy-start.3
  401.6 1.7 copy-start.2
